TPU v7x, 32 devices: a whole 2x2x4 slice. The times are simulated.
32 devices in a mesh: expert: 4 (over y, x), context: 8 (over z, core).
Axes of the slice: x: 2, y: 2, z: 4, core: 2. Of those that a mesh axis runs over, the one named last changes fastest.
Arguments:
- tokens: bfloat16 [4, 1024, 768], P('expert', 'context'), may hold values from -6 to 6
- segments: int32 [4, 1024], P('expert', 'context'), may hold values from 0 to 15, never falling along the last dimension, each value on 1 to 512 neighbouring positions
- routes: int32 [4, 1024, 2], P('expert', 'context'), may hold values from 0 to 7, all different within a row
- attn_gain: bfloat16 [768], replicated, may hold values from 0.5 to 1.5
- w_query: bfloat16 [768, 768], replicated, may hold values from -0.21875 to 0.21875
- w_key: bfloat16 [768, 768], replicated, may hold values from -0.21875 to 0.21875
- w_value: bfloat16 [768, 768], replicated, may hold values from -0.21875 to 0.21875
- w_out: bfloat16 [768, 768], replicated, may hold values from -1.25 to 1.25
- ffn_gain: bfloat16 [768], replicated, may hold values from 0.5 to 1.5
- w_router: bfloat16 [768, 8], replicated, may hold values from -0.21875 to 0.21875
- shared_gate: bfloat16 [768, 2048], replicated, may hold values from -0.21875 to 0.21875
- shared_up: bfloat16 [768, 2048], replicated, may hold values from -0.21875 to 0.21875
- shared_down: bfloat16 [2048, 768], replicated, may hold values from -0.125 to 0.125
- expert_gate: bfloat16 [8, 768, 2048], P('expert'), may hold values from -0.21875 to 0.21875
- expert_up: bfloat16 [8, 768, 2048], P('expert'), may hold values from -0.21875 to 0.21875
- expert_down: bfloat16 [8, 2048, 768], P('expert'), may hold values from -0.125 to 0.125
- cotangent: bfloat16 [4, 1024, 768], P('expert', 'context'), may hold values from -6 to 6
Outputs:
- result: bfloat16 [4, 1024, 768], P('expert', 'context')
- d_tokens: float32 [4, 1024, 768], P('expert', 'context')
- grad_attn_gain: float32 [768], replicated
- grad_w_query: float32 [768, 768], replicated
- grad_w_key: float32 [768, 768], replicated
- grad_w_value: float32 [768, 768], replicated
- grad_w_out: float32 [768, 768], replicated
- grad_ffn_gain: float32 [768], replicated
- grad_w_router: float32 [768, 8], replicated
- grad_shared_gate: float32 [768, 2048], replicated
- grad_shared_up: float32 [768, 2048], replicated
- grad_shared_down: float32 [2048, 768], replicated
- grad_expert_gate: float32 [8, 768, 2048], P('expert')
- grad_expert_up: float32 [8, 768, 2048], P('expert')
- grad_expert_down: float32 [8, 2048, 768], P('expert')
Inputs may be any that keep to these rules, and one draw needn't show every extreme that they name: `segments`: segment numbers never fall along a sequence; a document spans at most half of 1024 positions. A token's 2 routes name different experts.
All inputs are finite; a program needn't handle non-finite values.
Results may differ from a plain program's by a relative error of at most 0.025.
Values may be sent and summed in bfloat16 or wider, within the bound.
No kernel may reach another device: no remote copies, remote signals or barrier semaphores. Data moves between devices by JAX's collectives and lax.ppermute only.
A program may use at most 320 MiB of HBM per device.

v0:
```python
import math

import jax
import jax.numpy as jnp
from jax import lax
from jax.sharding import PartitionSpec as P

HEADS = 12
HEAD = 64
TOP = 2


EPSILON = 1e-06
MASKED = -1e30
HIGHEST = lax.Precision.HIGHEST


def rope_table(positions, head_dim):
    half_dim = head_dim // 2
    frequency = jnp.exp(
        jnp.arange(half_dim, dtype=jnp.float32) * (-2.0 * math.log(10000.0) / head_dim)
    )
    angles = positions.astype(jnp.float32)[:, None] * frequency[None, :]
    return (jnp.cos(angles), jnp.sin(angles))


def rotate(values, cosines, sine_table, turning):
    half_dim = values.shape[-1] // 2
    former = values[..., :half_dim]
    latter = values[..., half_dim:]
    cos_part = cosines[:, None, :]
    sin_part = turning * sine_table[:, None, :]
    return jnp.concatenate(
        [former * cos_part - latter * sin_part, latter * cos_part + former * sin_part], -1
    )


def block_span(length_now, stretch_len):
    return stretch_len * math.gcd(length_now // stretch_len, max(1, 1024 // stretch_len))


def masked_scores(queries, keys, seg_query, seg_key, pos_query, pos_key):
    scores = jnp.einsum(
        "sqhd,skhd->shqk", queries, keys, preferred_element_type=jnp.float32
    ) * HEAD ** (-0.5)
    allowed = (seg_query[:, None, :, None] == seg_key[:, None, None, :]) & (
        pos_key[None, None, None, :] <= pos_query[None, None, :, None]
    )
    return (scores, allowed)


def score_grads(
    queries, keys, values, d_attended, log_sum, delta, seg_query, seg_key, pos_query, pos_key
):
    scores, allowed = masked_scores(queries, keys, seg_query, seg_key, pos_query, pos_key)
    probs_now = jnp.where(allowed, jnp.exp(scores - jnp.swapaxes(log_sum, 1, 2)[..., None]), 0.0)
    d_probs = jnp.einsum("sqhd,skhd->shqk", d_attended, values, preferred_element_type=jnp.float32)
    d_scores = (probs_now * (d_probs - jnp.swapaxes(delta, 1, 2)[..., None])).astype(jnp.bfloat16)
    return (probs_now.astype(jnp.bfloat16), d_scores)


def silu_slope(values):
    sigmoid_v = jax.nn.sigmoid(values)
    return sigmoid_v * (1.0 + values * (1.0 - sigmoid_v))


def per_device(
    tokens,
    segments,
    routes,
    attn_gain,
    w_query,
    w_key,
    w_value,
    w_out,
    ffn_gain,
    w_router,
    shared_gate,
    shared_up,
    shared_down,
    expert_gate,
    expert_up,
    expert_down,
    cotangent,
):
    seq_count, stretch_len, model_width = tokens.shape
    row_count = seq_count * stretch_len
    owner_count = lax.axis_size("expert")
    local_experts = expert_gate.shape[0]
    expert_count = owner_count * local_experts
    capacity = (9 * row_count * TOP + 8 * expert_count - 1) // (8 * expert_count)
    score_scale = HEAD ** (-0.5)
    query_pos = lax.axis_index("context") * stretch_len + jnp.arange(stretch_len, dtype=jnp.int32)
    cosines, sine_table = rope_table(query_pos, HEAD)
    shape4 = (seq_count, stretch_len, HEADS, HEAD)
    layer_inputs = tokens.astype(jnp.float32)
    rstd_a = lax.rsqrt(jnp.mean(layer_inputs * layer_inputs, -1, keepdims=True) + EPSILON)
    normed_a = layer_inputs * rstd_a
    attention_norm_gain = attn_gain.astype(jnp.float32)
    low_a = (normed_a * attention_norm_gain).astype(jnp.bfloat16)
    q_pre = jnp.einsum("scd,de->sce", low_a, w_query, preferred_element_type=jnp.float32).reshape(
        shape4
    )
    k_pre = jnp.einsum("scd,de->sce", low_a, w_key, preferred_element_type=jnp.float32).reshape(
        shape4
    )
    queries = rotate(q_pre, cosines, sine_table, 1.0).astype(jnp.bfloat16)
    keys = rotate(k_pre, cosines, sine_table, 1.0).astype(jnp.bfloat16)
    values = (
        jnp.einsum("scd,de->sce", low_a, w_value, preferred_element_type=jnp.float32)
        .astype(jnp.bfloat16)
        .reshape(shape4)
    )
    start_state = (
        jnp.full((seq_count, HEADS, stretch_len), MASKED, jnp.float32),
        jnp.zeros((seq_count, HEADS, stretch_len), jnp.float32),
        jnp.zeros(shape4, jnp.float32),
    )
    key_piece = lax.all_gather(keys, "context", axis=1, tiled=True)
    value_piece = lax.all_gather(values, "context", axis=1, tiled=True)
    seg_piece = lax.all_gather(segments, "context", axis=1, tiled=True)
    fold_block_len = block_span(key_piece.shape[1], stretch_len)

    def advance(step_index, inner):
        running_max, running_sum, accumulated = inner
        offset = step_index * fold_block_len
        key_block = lax.dynamic_slice_in_dim(key_piece, offset, fold_block_len, 1)
        value_block = lax.dynamic_slice_in_dim(value_piece, offset, fold_block_len, 1)
        seg_block = lax.dynamic_slice_in_dim(seg_piece, offset, fold_block_len, 1)
        key_pos = offset + jnp.arange(fold_block_len, dtype=jnp.int32)
        scores, allowed = masked_scores(queries, key_block, segments, seg_block, query_pos, key_pos)
        scores = jnp.where(allowed, scores, MASKED)
        new_max = jnp.maximum(running_max, jnp.max(scores, -1))
        shrink = jnp.exp(running_max - new_max)
        weights_now = jnp.where(allowed, jnp.exp(scores - new_max[..., None]), 0.0)
        running_sum = running_sum * shrink + jnp.sum(weights_now, -1)
        accumulated = accumulated * jnp.swapaxes(shrink, 1, 2)[..., None] + jnp.einsum(
            "shqk,skhd->sqhd",
            weights_now.astype(jnp.bfloat16),
            value_block,
            preferred_element_type=jnp.float32,
        )
        return (new_max, running_sum, accumulated)

    row_max, row_sum, accumulated = lax.fori_loop(
        0, key_piece.shape[1] // fold_block_len, advance, start_state
    )
    log_sum = jnp.swapaxes(row_max + jnp.log(row_sum), 1, 2)
    attended_f = accumulated / jnp.swapaxes(row_sum, 1, 2)[..., None]
    attended = attended_f.astype(jnp.bfloat16).reshape(seq_count, stretch_len, model_width)
    hidden1 = layer_inputs + jnp.einsum(
        "scd,de->sce", attended, w_out, preferred_element_type=jnp.float32
    )
    rstd_b = lax.rsqrt(jnp.mean(hidden1 * hidden1, -1, keepdims=True) + EPSILON)
    normed_b = hidden1 * rstd_b
    feed_norm_gain = ffn_gain.astype(jnp.float32)
    low_b = (normed_b * feed_norm_gain).astype(jnp.bfloat16)
    gate_sh = jnp.einsum("scd,df->scf", low_b, shared_gate, preferred_element_type=jnp.float32)
    up_sh = jnp.einsum("scd,df->scf", low_b, shared_up, preferred_element_type=jnp.float32)
    hidden_sh = (jax.nn.silu(gate_sh) * up_sh).astype(jnp.bfloat16)
    shared_out = jnp.einsum(
        "scf,fd->scd", hidden_sh, shared_down, preferred_element_type=jnp.float32
    )
    logits = jnp.einsum("scd,de->sce", low_b, w_router, preferred_element_type=jnp.float32)
    gates = jax.nn.softmax(jnp.take_along_axis(logits, routes, -1), -1)
    assigned = routes.reshape(row_count * TOP)
    onehot = (assigned[:, None] == jnp.arange(expert_count, dtype=jnp.int32)[None, :]).astype(
        jnp.int32
    )
    before = jnp.cumsum(onehot, 0) - onehot
    place = jnp.sum(before * onehot, -1)
    slot = jnp.where(place < capacity, assigned * capacity + place, expert_count * capacity)
    order = (
        jnp.zeros((expert_count * capacity + 1,), jnp.int32)
        .at[slot]
        .set(jnp.arange(row_count * TOP, dtype=jnp.int32))[: expert_count * capacity]
    )
    filled = (
        jnp.zeros((expert_count * capacity + 1,), jnp.int32)
        .at[slot]
        .set(1)[: expert_count * capacity]
        > 0
    )
    buffer_shape = (owner_count, local_experts, capacity, model_width)
    flat_b = low_b.reshape(row_count, model_width)
    outgoing = jnp.where(
        filled[:, None], flat_b[order // TOP], jnp.zeros((), jnp.bfloat16)
    ).reshape(buffer_shape)
    received = lax.all_to_all(outgoing, "expert", split_axis=0, concat_axis=0, tiled=True)
    gate_ex = jnp.einsum(
        "secd,edf->secf", received, expert_gate, preferred_element_type=jnp.float32
    )
    up_ex = jnp.einsum("secd,edf->secf", received, expert_up, preferred_element_type=jnp.float32)
    hidden_ex = (jax.nn.silu(gate_ex) * up_ex).astype(jnp.bfloat16)
    out_ex = jnp.einsum(
        "secf,efd->secd", hidden_ex, expert_down, preferred_element_type=jnp.float32
    ).astype(jnp.bfloat16)
    returned = lax.all_to_all(out_ex, "expert", split_axis=0, concat_axis=0, tiled=True).reshape(
        expert_count * capacity, model_width
    )
    back_rows = (
        jnp.take(returned, slot, axis=0, mode="fill", fill_value=0)
        .reshape(seq_count, stretch_len, TOP, model_width)
        .astype(jnp.float32)
    )
    moe_out = jnp.sum(gates[..., None] * back_rows, 2)
    result = (hidden1 + shared_out + moe_out).astype(jnp.bfloat16)
    grad_in = cotangent.astype(jnp.float32)
    g_shared_down = jnp.einsum(
        "scf,scd->fd", hidden_sh, cotangent, preferred_element_type=jnp.float32
    )
    d_hidden_sh = jnp.einsum(
        "scd,fd->scf", cotangent, shared_down, preferred_element_type=jnp.float32
    )
    d_gate_sh = (d_hidden_sh * up_sh * silu_slope(gate_sh)).astype(jnp.bfloat16)
    d_up_sh = (d_hidden_sh * jax.nn.silu(gate_sh)).astype(jnp.bfloat16)
    g_shared_gate = jnp.einsum("scd,scf->df", low_b, d_gate_sh, preferred_element_type=jnp.float32)
    g_shared_up = jnp.einsum("scd,scf->df", low_b, d_up_sh, preferred_element_type=jnp.float32)
    d_b = jnp.einsum("scf,df->scd", d_gate_sh, shared_gate, preferred_element_type=jnp.float32)
    d_b = d_b + jnp.einsum("scf,df->scd", d_up_sh, shared_up, preferred_element_type=jnp.float32)
    d_gates = jnp.sum(grad_in[:, :, None, :] * back_rows, -1)
    d_chosen = gates * (d_gates - jnp.sum(gates * d_gates, -1, keepdims=True))
    route_hot = (routes[..., None] == jnp.arange(expert_count, dtype=jnp.int32)).astype(jnp.float32)
    d_logits = jnp.sum(d_chosen[..., None] * route_hot, 2)
    g_router = jnp.einsum("scd,sce->de", low_b.astype(jnp.float32), d_logits, precision=HIGHEST)
    d_b = d_b + jnp.einsum("sce,de->scd", d_logits, w_router.astype(jnp.float32), precision=HIGHEST)
    d_rows = (
        (gates[..., None] * grad_in[:, :, None, :])
        .astype(jnp.bfloat16)
        .reshape(row_count * TOP, model_width)
    )
    grad_out = jnp.where(filled[:, None], d_rows[order], jnp.zeros((), jnp.bfloat16)).reshape(
        buffer_shape
    )
    d_out_ex = lax.all_to_all(grad_out, "expert", split_axis=0, concat_axis=0, tiled=True)
    g_expert_down = jnp.einsum(
        "secf,secd->efd", hidden_ex, d_out_ex, preferred_element_type=jnp.float32
    )
    d_hidden_ex = jnp.einsum(
        "secd,efd->secf", d_out_ex, expert_down, preferred_element_type=jnp.float32
    )
    d_gate_ex = (d_hidden_ex * up_ex * silu_slope(gate_ex)).astype(jnp.bfloat16)
    d_up_ex = (d_hidden_ex * jax.nn.silu(gate_ex)).astype(jnp.bfloat16)
    g_expert_gate = jnp.einsum(
        "secd,secf->edf", received, d_gate_ex, preferred_element_type=jnp.float32
    )
    g_expert_up = jnp.einsum(
        "secd,secf->edf", received, d_up_ex, preferred_element_type=jnp.float32
    )
    d_received = jnp.einsum(
        "secf,edf->secd", d_gate_ex, expert_gate, preferred_element_type=jnp.float32
    )
    d_received = (
        d_received
        + jnp.einsum("secf,edf->secd", d_up_ex, expert_up, preferred_element_type=jnp.float32)
    ).astype(jnp.bfloat16)
    d_sent = lax.all_to_all(d_received, "expert", split_axis=0, concat_axis=0, tiled=True).reshape(
        expert_count * capacity, model_width
    )
    d_back = (
        jnp.take(d_sent, slot, axis=0, mode="fill", fill_value=0)
        .reshape(seq_count, stretch_len, TOP, model_width)
        .astype(jnp.float32)
    )
    d_b = d_b + jnp.sum(d_back, 2)
    g_ffn_gain = jnp.sum(d_b * normed_b, (0, 1))
    d_nb = d_b * feed_norm_gain
    d_h1 = grad_in + rstd_b * (d_nb - normed_b * jnp.mean(d_nb * normed_b, -1, keepdims=True))
    d_attn = d_h1.astype(jnp.bfloat16)
    g_out = jnp.einsum("scd,sce->de", attended, d_attn, preferred_element_type=jnp.float32)
    d_attended = (
        jnp.einsum("sce,de->scd", d_attn, w_out, preferred_element_type=jnp.float32)
        .astype(jnp.bfloat16)
        .reshape(shape4)
    )
    delta = jnp.sum(d_attended.astype(jnp.float32) * attended_f, -1)
    zeros4 = jnp.zeros(shape4, jnp.float32)
    whole_keys, whole_values, whole_segs = (
        lax.all_gather(keys, "context", axis=1, tiled=True),
        lax.all_gather(values, "context", axis=1, tiled=True),
        lax.all_gather(segments, "context", axis=1, tiled=True),
    )
    block_len = block_span(whole_keys.shape[1], stretch_len)
    parts_per = block_len // stretch_len

    def term_step(grad_query, step_index):
        offset = step_index * block_len
        key_block = lax.dynamic_slice_in_dim(whole_keys, offset, block_len, 1)
        value_block = lax.dynamic_slice_in_dim(whole_values, offset, block_len, 1)
        seg_block = lax.dynamic_slice_in_dim(whole_segs, offset, block_len, 1)
        key_pos = offset + jnp.arange(block_len, dtype=jnp.int32)
        probs_low, d_scores = score_grads(
            queries,
            key_block,
            value_block,
            d_attended,
            log_sum,
            delta,
            segments,
            seg_block,
            query_pos,
            key_pos,
        )
        grad_query = grad_query + score_scale * jnp.einsum(
            "shqk,skhd->sqhd", d_scores, key_block, preferred_element_type=jnp.float32
        )
        shape5 = d_scores.shape[:3] + (parts_per, stretch_len)
        key_term = score_scale * jnp.einsum(
            "shqrc,sqhd->rschd",
            d_scores.reshape(shape5),
            queries,
            preferred_element_type=jnp.float32,
        )
        value_term = jnp.einsum(
            "shqrc,sqhd->rschd",
            probs_low.reshape(shape5),
            d_attended,
            preferred_element_type=jnp.float32,
        )
        return (grad_query, (key_term, value_term))

    d_queries, terms = lax.scan(term_step, zeros4, jnp.arange(whole_keys.shape[1] // block_len))
    key_sum, value_sum = (
        lax.psum_scatter(
            terms[0].reshape((-1,) + shape4).astype(jnp.bfloat16),
            "context",
            scatter_dimension=0,
            tiled=True,
        ).astype(jnp.float32),
        lax.psum_scatter(
            terms[1].reshape((-1,) + shape4).astype(jnp.bfloat16),
            "context",
            scatter_dimension=0,
            tiled=True,
        ).astype(jnp.float32),
    )
    d_keys = key_sum[0]
    d_values = value_sum[0]
    d_q_pre = (
        rotate(d_queries, cosines, sine_table, -1.0)
        .astype(jnp.bfloat16)
        .reshape(seq_count, stretch_len, model_width)
    )
    d_k_pre = (
        rotate(d_keys, cosines, sine_table, -1.0)
        .astype(jnp.bfloat16)
        .reshape(seq_count, stretch_len, model_width)
    )
    d_v_low = d_values.astype(jnp.bfloat16).reshape(seq_count, stretch_len, model_width)
    g_query = jnp.einsum("scd,sce->de", low_a, d_q_pre, preferred_element_type=jnp.float32)
    g_key = jnp.einsum("scd,sce->de", low_a, d_k_pre, preferred_element_type=jnp.float32)
    g_value = jnp.einsum("scd,sce->de", low_a, d_v_low, preferred_element_type=jnp.float32)
    d_a = jnp.einsum("sce,de->scd", d_q_pre, w_query, preferred_element_type=jnp.float32)
    d_a = d_a + jnp.einsum("sce,de->scd", d_k_pre, w_key, preferred_element_type=jnp.float32)
    d_a = d_a + jnp.einsum("sce,de->scd", d_v_low, w_value, preferred_element_type=jnp.float32)
    g_attn_gain = jnp.sum(d_a * normed_a, (0, 1))
    d_na = d_a * attention_norm_gain
    d_tokens = d_h1 + rstd_a * (d_na - normed_a * jnp.mean(d_na * normed_a, -1, keepdims=True))
    dense_parts = (
        lax.psum_scatter(
            g_attn_gain.astype(jnp.bfloat16), "context", scatter_dimension=0, tiled=True
        ).astype(jnp.float32),
        lax.psum_scatter(
            g_query.astype(jnp.bfloat16), "context", scatter_dimension=0, tiled=True
        ).astype(jnp.float32),
        lax.psum_scatter(
            g_key.astype(jnp.bfloat16), "context", scatter_dimension=0, tiled=True
        ).astype(jnp.float32),
        lax.psum_scatter(
            g_value.astype(jnp.bfloat16), "context", scatter_dimension=0, tiled=True
        ).astype(jnp.float32),
        lax.psum_scatter(
            g_out.astype(jnp.bfloat16), "context", scatter_dimension=0, tiled=True
        ).astype(jnp.float32),
        lax.psum_scatter(
            g_ffn_gain.astype(jnp.bfloat16), "context", scatter_dimension=0, tiled=True
        ).astype(jnp.float32),
        lax.psum_scatter(
            g_router.astype(jnp.bfloat16), "context", scatter_dimension=0, tiled=True
        ).astype(jnp.float32),
        lax.psum_scatter(
            g_shared_gate.astype(jnp.bfloat16), "context", scatter_dimension=0, tiled=True
        ).astype(jnp.float32),
        lax.psum_scatter(
            g_shared_up.astype(jnp.bfloat16), "context", scatter_dimension=0, tiled=True
        ).astype(jnp.float32),
        lax.psum_scatter(
            g_shared_down.astype(jnp.bfloat16), "context", scatter_dimension=0, tiled=True
        ).astype(jnp.float32),
    )
    dense_total = (
        lax.psum(dense_parts[0].astype(jnp.bfloat16), "expert").astype(jnp.float32),
        lax.psum(dense_parts[1].astype(jnp.bfloat16), "expert").astype(jnp.float32),
        lax.psum(dense_parts[2].astype(jnp.bfloat16), "expert").astype(jnp.float32),
        lax.psum(dense_parts[3].astype(jnp.bfloat16), "expert").astype(jnp.float32),
        lax.psum(dense_parts[4].astype(jnp.bfloat16), "expert").astype(jnp.float32),
        lax.psum(dense_parts[5].astype(jnp.bfloat16), "expert").astype(jnp.float32),
        lax.psum(dense_parts[6].astype(jnp.bfloat16), "expert").astype(jnp.float32),
        lax.psum(dense_parts[7].astype(jnp.bfloat16), "expert").astype(jnp.float32),
        lax.psum(dense_parts[8].astype(jnp.bfloat16), "expert").astype(jnp.float32),
        lax.psum(dense_parts[9].astype(jnp.bfloat16), "expert").astype(jnp.float32),
    )
    dense = (
        lax.all_gather(dense_total[0].astype(jnp.bfloat16), "context", axis=0, tiled=True).astype(
            jnp.float32
        ),
        lax.all_gather(dense_total[1].astype(jnp.bfloat16), "context", axis=0, tiled=True).astype(
            jnp.float32
        ),
        lax.all_gather(dense_total[2].astype(jnp.bfloat16), "context", axis=0, tiled=True).astype(
            jnp.float32
        ),
        lax.all_gather(dense_total[3].astype(jnp.bfloat16), "context", axis=0, tiled=True).astype(
            jnp.float32
        ),
        lax.all_gather(dense_total[4].astype(jnp.bfloat16), "context", axis=0, tiled=True).astype(
            jnp.float32
        ),
        lax.all_gather(dense_total[5].astype(jnp.bfloat16), "context", axis=0, tiled=True).astype(
            jnp.float32
        ),
        lax.all_gather(dense_total[6].astype(jnp.bfloat16), "context", axis=0, tiled=True).astype(
            jnp.float32
        ),
        lax.all_gather(dense_total[7].astype(jnp.bfloat16), "context", axis=0, tiled=True).astype(
            jnp.float32
        ),
        lax.all_gather(dense_total[8].astype(jnp.bfloat16), "context", axis=0, tiled=True).astype(
            jnp.float32
        ),
        lax.all_gather(dense_total[9].astype(jnp.bfloat16), "context", axis=0, tiled=True).astype(
            jnp.float32
        ),
    )
    expert_parts = (
        lax.psum_scatter(
            g_expert_gate.astype(jnp.bfloat16), "context", scatter_dimension=1, tiled=True
        ).astype(jnp.float32),
        lax.psum_scatter(
            g_expert_up.astype(jnp.bfloat16), "context", scatter_dimension=1, tiled=True
        ).astype(jnp.float32),
        lax.psum_scatter(
            g_expert_down.astype(jnp.bfloat16), "context", scatter_dimension=1, tiled=True
        ).astype(jnp.float32),
    )
    expert_grads = (
        lax.all_gather(expert_parts[0].astype(jnp.bfloat16), "context", axis=1, tiled=True).astype(
            jnp.float32
        ),
        lax.all_gather(expert_parts[1].astype(jnp.bfloat16), "context", axis=1, tiled=True).astype(
            jnp.float32
        ),
        lax.all_gather(expert_parts[2].astype(jnp.bfloat16), "context", axis=1, tiled=True).astype(
            jnp.float32
        ),
    )
    return (
        result,
        d_tokens,
        dense[0],
        dense[1],
        dense[2],
        dense[3],
        dense[4],
        dense[5],
        dense[6],
        dense[7],
        dense[8],
        dense[9],
        expert_grads[0],
        expert_grads[1],
        expert_grads[2],
    )


def solution(mesh):
    placed = (
        P("expert", "context", None),
        P("expert", "context"),
        P("expert", "context", None),
        P(),
        P(),
        P(),
        P(),
        P(),
        P(),
        P(),
        P(),
        P(),
        P(),
        P("expert", None, None),
        P("expert", None, None),
        P("expert", None, None),
        P("expert", "context", None),
    )
    return jax.shard_map(
        per_device,
        mesh=mesh,
        in_specs=placed,
        out_specs=(
            P("expert", "context", None),
            P("expert", "context", None),
            P(),
            P(),
            P(),
            P(),
            P(),
            P(),
            P(),
            P(),
            P(),
            P(),
            P("expert", None, None),
            P("expert", None, None),
            P("expert", None, None),
        ),
        check_vma=False,
    )
```

profile of v0, /device:TPU:0, one launch (start us, length us, event | category | flops | bytes accessed | tf_op | source)
XLA Modules:
  0.0 1324.4 jit_solution(11107535247798729818)
XLA Ops:
  47.5 13.7 %all_gather.53 = s32[1,1024]{1,0:T(1,128)S(1)} all-gather(s32[1,128]{1,0:T(1,128)} %param.20), channel_id=1, replica_groups=mesh['expert'=4,'context'=8] {'context'}, dimensions={1}, use_global_device_ids=true | all-gather | bytes 4608 | tf_op jit(solution)/shard_map/all_gather | solution.py:121
  70.7 8.3 all-gather.16.cloned.1.call-done
  79.0 5.9 fusion.160
  93.1 4.3 all-to-all-start
  107.6 4.3 fusion.28
  112.0 7.0 multiply_convert_fusion.4
  121.5 4.2 all-to-all-start.1
  126.2 4.0 fusion.164
  130.2 3.3 all-to-all-done.1
  137.2 3.4 gather_fusion.3
  149.9 4.0 gather_fusion.1
  158.0 4.6 all-to-all-start.2
  162.6 4.0 convolution_add_fusion.3
  166.6 2.9 all-to-all-done.2
  169.5 6.8 multiply_convert_fusion.3
  176.3 5.9 fusion
  182.3 5.0 fusion.64
  188.5 4.1 all-to-all-start.3
  193.4 5.5 all-to-all-done.3
  202.6 3.3 gather_fusion.4
  222.8 5.5 fusion.46
  229.8 5.8 multiply_convert_fusion
  243.2 47.5 %all-reduce.12.cloned.1.call-done = bf16[8,1,128,12,64]{2,4,0,3,1:T(8,128)(2,1)} async-done(((bf16[8,1,128,12,64]{2,4,0,3,1:T(8,128)(2,1)}), bf16[8,1,128,12,64]{2,4,0,3,1:T(8,128)(2,1)}) %all-reduce.12.cloned.1.call-update) | async-done | bytes 1572880
  294.6 3.7 convolution_convert_fusion.1
  298.4 3.7 convolution_convert_fusion.2
  302.2 3.8 convolution_convert_fusion
  306.0 4.3 fusion.71
  310.4 16.4 %reduce-scatter.18.cloned.1.call-done = bf16[1,1,128,12,64]{2,4,3,1,0:T(8,128)(2,1)} async-done(((bf16[8,1,128,12,64]{2,4,3,1,0:T(8,128)(2,1)}), bf16[1,1,128,12,64]{2,4,3,1,0:T(8,128)(2,1)}) %reduce-scatter.18.cloned.1.call-update) | async-done | bytes 196624 | tf_op jit(solution)/shard_map/reduce_scatter | solution.py:324
  335.3 24.4 %reduce-scatter.26.cloned.1.call-done = bf16[96,768]{1,0:T(8,128)(2,1)} async-done(((bf16[768,768]{1,0:T(8,128)(2,1)}), bf16[96,768]{1,0:T(8,128)(2,1)}) %reduce-scatter.26.cloned.1.call-update) | async-done | bytes 147472 | tf_op jit(solution)/shard_map/reduce_scatter | solution.py:372
  359.7 33.7 %reduce-scatter.24.cloned.1.call-done = bf16[96,768]{1,0:T(8,128)(2,1)} async-done(((bf16[768,768]{1,0:T(8,128)(2,1)}), bf16[96,768]{1,0:T(8,128)(2,1)}) %reduce-scatter.24.cloned.1.call-update) | async-done | bytes 147472 | tf_op jit(solution)/shard_map/reduce_scatter | solution.py:369
  393.4 41.4 %reduce-scatter.30.cloned.1.call-done = bf16[96,2048]{1,0:T(8,128)(2,1)} async-done(((bf16[768,2048]{1,0:T(8,128)(2,1)}), bf16[96,2048]{1,0:T(8,128)(2,1)}) %reduce-scatter.30.cloned.1.call-update) | async-done | bytes 393232 | tf_op jit(solution)/shard_map/reduce_scatter | solution.py:384
  434.8 42.3 %reduce-scatter.28.cloned.1.call-done = bf16[96,2048]{1,0:T(8,128)(2,1)} async-done(((bf16[768,2048]{1,0:T(8,128)(2,1)}), bf16[96,2048]{1,0:T(8,128)(2,1)}) %reduce-scatter.28.cloned.1.call-update) | async-done | bytes 393232 | tf_op jit(solution)/shard_map/reduce_scatter | solution.py:381
  477.1 42.4 %reduce-scatter.32.cloned.1.call-done = bf16[256,768]{1,0:T(8,128)(2,1)} async-done(((bf16[2048,768]{1,0:T(8,128)(2,1)}), bf16[256,768]{1,0:T(8,128)(2,1)}) %reduce-scatter.32.cloned.1.call-update) | async-done | bytes 393232 | tf_op jit(solution)/shard_map/reduce_scatter | solution.py:387
  519.4 34.6 %reduce-scatter.22.cloned.1.call-done = bf16[96,768]{1,0:T(8,128)(2,1)} async-done(((bf16[768,768]{1,0:T(8,128)(2,1)}), bf16[96,768]{1,0:T(8,128)(2,1)}) %reduce-scatter.22.cloned.1.call-update) | async-done | bytes 147472 | tf_op jit(solution)/shard_map/reduce_scatter | solution.py:366
  554.1 33.9 %reduce-scatter.20.cloned.1.call-done = bf16[96,768]{1,0:T(8,128)(2,1)} async-done(((bf16[768,768]{1,0:T(8,128)(2,1)}), bf16[96,768]{1,0:T(8,128)(2,1)}) %reduce-scatter.20.cloned.1.call-update) | async-done | bytes 147472 | tf_op jit(solution)/shard_map/reduce_scatter | solution.py:363
  588.0 6.0 bitcast_convert_fusion.1
  594.4 6.4 bitcast_convert_fusion.2
  600.8 6.1 bitcast_convert_fusion
  609.3 46.1 %all-reduce.14.cloned.1.call-done = (bf16[96,768]{1,0:T(8,128)(2,1)}, bf16[96,768]{1,0:T(8,128)(2,1)}, bf16[96,768]{1,0:T(8,128)(2,1)}, bf16[96,768]{1,0:T(8,128...) async-done(((bf16[96,768]{1,0:T(8,128)(2,1)}, bf16[96,768]{1,0:T(8,128)(2,1)}, bf16[96,768]{1,0:T(8,128)(2,1)}, ...) | async-done | bytes 1769488 | tf_op jit(solution)/shard_map/psum | solution.py:393
  659.7 68.5 %reduce-scatter.36.cloned.1.call-done = bf16[2,96,2048]{2,1,0:T(8,128)(2,1)} async-done(((bf16[2,768,2048]{2,1,0:T(8,128)(2,1)}), bf16[2,96,2048]{2,1,0:T(8,128)(2,1)}) %reduce-scatter.36.cloned.1.call-update) | async-done | bytes 786448 | tf_op jit(solution)/shard_map/reduce_scatter | solution.py:439
  728.2 70.8 %reduce-scatter.34.cloned.1.call-done = bf16[2,96,2048]{2,1,0:T(8,128)(2,1)} async-done(((bf16[2,768,2048]{2,1,0:T(8,128)(2,1)}), bf16[2,96,2048]{2,1,0:T(8,128)(2,1)}) %reduce-scatter.34.cloned.1.call-update) | async-done | bytes 786448 | tf_op jit(solution)/shard_map/reduce_scatter | solution.py:436
  799.2 70.9 %reduce-scatter.38.cloned.1.call-done = bf16[2,256,768]{2,1,0:T(8,128)(2,1)} async-done(((bf16[2,2048,768]{2,1,0:T(8,128)(2,1)}), bf16[2,256,768]{2,1,0:T(8,128)(2,1)}) %reduce-scatter.38.cloned.1.call-update) | async-done | bytes 786448 | tf_op jit(solution)/shard_map/reduce_scatter | solution.py:442
  871.4 30.0 %reduce-scatter.40.cloned.1.call-done = bf16[96,8]{1,0:T(8,128)(2,1)} async-done(((bf16[768,8]{1,0:T(8,128)(2,1)}), bf16[96,8]{1,0:T(8,128)(2,1)}) %reduce-scatter.40.cloned.1.call-update) | async-done | bytes 1552
  912.0 13.8 %all-reduce.6 = (bf16[768]{0:T(1024)(128)(2,1)S(1)}, bf16[768]{0:T(1024)(128)(2,1)S(1)}) all-reduce(bf16[768]{0:T(1024)(128)(2,1)S(1)} %get-tuple-element.77, bf16[768]{0:T(1024)(128)(2,1)S(1)} %copy-done.43), channel_id=4, replica_groups=mesh['expert'=4,'context'=8] {'context'}, use_global_device_ids=true, to_apply=%region_22.24.clone | all-reduce | flops 1536 | bytes 6144
  926.0 10.1 all-reduce.7
  936.5 13.8 %all-reduce.5 = (bf16[768]{0:T(1024)(128)(2,1)S(1)}, bf16[768]{0:T(1024)(128)(2,1)S(1)}) all-reduce(bf16[768]{0:T(1024)(128)(2,1)S(1)} %dynamic-update-slice, bf16[768]{0:T(1024)(128)(2,1)S(1)} %dynamic-update-slice.1), channel_id=1, replica_groups=mesh['expert'=4,'context'=8] {'context'}, use_global_device_ids=true, to_apply=%add | all-reduce | flops 1536 | bytes 6144
  951.5 13.0 all-gather
  967.2 2.9 convert_element_type.428
  970.1 2.8 convert_element_type.426
  972.9 2.8 convert_element_type.424
  975.8 20.3 %all-gather.18.cloned.1.call-done = bf16[768,768]{1,0:T(8,128)(2,1)} async-done(((bf16[96,768]{1,0:T(8,128)(2,1)}), bf16[768,768]{1,0:T(8,128)(2,1)}) %all-gather.18.cloned.1.call-update) | async-done | bytes 1179664 | tf_op jit(solution)/shard_map/all_gather | solution.py:407
  996.1 2.8 convert_element_type.422
  998.9 37.0 %all-gather.30.cloned.1.call-done = bf16[2048,768]{1,0:T(8,128)(2,1)} async-done(((bf16[256,768]{1,0:T(8,128)(2,1)}), bf16[2048,768]{1,0:T(8,128)(2,1)}) %all-gather.30.cloned.1.call-update) | async-done | bytes 3145744 | tf_op jit(solution)/shard_map/all_gather | solution.py:431
  1035.9 5.1 convert_element_type.438
  1041.0 33.8 %all-gather.28.cloned.1.call-done = bf16[768,2048]{1,0:T(8,128)(2,1)} async-done(((bf16[96,2048]{1,0:T(8,128)(2,1)}), bf16[768,2048]{1,0:T(8,128)(2,1)}) %all-gather.28.cloned.1.call-update) | async-done | bytes 3145744 | tf_op jit(solution)/shard_map/all_gather | solution.py:428
  1074.8 5.4 convert_element_type.436
  1080.3 33.5 %all-gather.26.cloned.1.call-done = bf16[768,2048]{1,0:T(8,128)(2,1)} async-done(((bf16[96,2048]{1,0:T(8,128)(2,1)}), bf16[768,2048]{1,0:T(8,128)(2,1)}) %all-gather.26.cloned.1.call-update) | async-done | bytes 3145744 | tf_op jit(solution)/shard_map/all_gather | solution.py:425
  1113.7 5.4 convert_element_type.434
  1119.2 59.7 %all-gather.34.cloned.1.call-done = bf16[2,768,2048]{2,1,0:T(8,128)(2,1)} async-done(((bf16[2,96,2048]{2,1,0:T(8,128)(2,1)}), bf16[2,768,2048]{2,1,0:T(8,128)(2,1)}) %all-gather.34.cloned.1.call-update) | async-done | bytes 6291472 | tf_op jit(solution)/shard_map/all_gather | solution.py:450
  1178.9 9.4 convert_element_type.442
  1188.3 55.7 %all-gather.32.cloned.1.call-done = bf16[2,768,2048]{2,1,0:T(8,128)(2,1)} async-done(((bf16[2,96,2048]{2,1,0:T(8,128)(2,1)}), bf16[2,768,2048]{2,1,0:T(8,128)(2,1)}) %all-gather.32.cloned.1.call-update) | async-done | bytes 6291472 | tf_op jit(solution)/shard_map/all_gather | solution.py:447
  1244.0 9.5 convert_element_type.440
  1253.5 55.5 %all-gather.36.cloned.1.call-done = bf16[2,2048,768]{2,1,0:T(8,128)(2,1)} async-done(((bf16[2,256,768]{2,1,0:T(8,128)(2,1)}), bf16[2,2048,768]{2,1,0:T(8,128)(2,1)}) %all-gather.36.cloned.1.call-update) | async-done | bytes 6291472 | tf_op jit(solution)/shard_map/all_gather | solution.py:453
  1309.0 8.6 convert_element_type.444
  (287 shorter events, 154.3 us)
Async XLA Ops:
  7.2 93.7 %copy-start = (bf16[2048,768]{1,0:T(8,128)(2,1)S(1)}, bf16[2048,768]{1,0:T(8,128)(2,1)}, u32[]{:S(2)}) copy-start(bf16[2048,768]{1,0:T(8,128)(2,1)} %param.31) | copy-start | bytes 9437188
  7.2 7.3 copy-start.2
  7.2 57.3 %all-gather.14.cloned.1.call-start = ((), (), s32[]{:S(2)}) async-start(), calls=%async_computation.16 | async-start | bytes 1769472 | tf_op jit(solution)/shard_map/all_gather | solution.py:119
  8.5 12.0 copy-start.32
  14.4 3.7 copy-start.47
  16.3 8.3 copy-start.34
  16.3 21.9 %copy-start.20 = (bf16[1,128,768]{2,1,0:T(8,128)(2,1)S(1)}, bf16[1,128,768]{2,1,0:T(8,128)(2,1)}, u32[]{:S(2)}) copy-start(bf16[1,128,768]{2,1,0:T(8,128)(2,1)} %param.35) | copy-start | bytes 589828
  20.4 58.5 %all-gather.16.cloned.1.call-start = ((), (), s32[]{:S(2)}) async-start(), calls=%async_computation.17 | async-start | bytes 1769472 | tf_op jit(solution)/shard_map/all_gather | solution.py:120
  26.3 12.6 copy-start.40
  40.3 45.1 %copy-start.29 = (f32[768]{0:T(1024)}, f32[768]{0:T(1024)S(1)}, u32[]{:S(2)}) copy-start(f32[768]{0:T(1024)S(1)} %convert_element_type.380) | copy-start | bytes 9220
  42.7 48.1 %copy-start.36 = (pred[4,2,36]{2,1,0:T(4,128)(4,1)}, pred[4,2,36]{2,1,0:T(4,128)(4,1)S(1)}, u32[]{:S(2)}) copy-start(pred[4,2,36]{2,1,0:T(4,128)(4,1)S(1)} %gt.8) | copy-start | bytes 868
  64.5 14.5 %copy-start.24 = (pred[128,1024]{1,0:T(8,128)(4,1)}, pred[128,1024]{1,0:T(8,128)(4,1)S(1)}, u32[]{:S(2)}) copy-start(pred[128,1024]{1,0:T(8,128)(4,1)S(1)} %fusion.98) | copy-start | bytes 393220
  79.0 5.9 copy-start.10
  93.1 14.5 %all-to-all-start = ((bf16[4,2,36,768]{3,1,2,0:T(2,128)(2,1)}), bf16[4,2,36,768]{3,1,2,0:T(2,128)(2,1)}, u32[]{:S(2)}, u32[]{:S(2)}) async-start(bf16[4,2,36,768]{3,1,2,0:T(2,128)(2,1)} %copy.136), calls=%async_computation | async-start | bytes 884736 | tf_op jit(solution)/shard_map/all_to_all | solution.py:189
  107.6 18.0 %copy-start.41 = (f32[1,128,2]{1,2,0:T(2,128)}, f32[1,128,2]{1,2,0:T(2,128)S(1)}, u32[]{:S(2)}) copy-start(f32[1,128,2]{1,2,0:T(2,128)S(1)} %get-tuple-element.109) | copy-start | bytes 3076
  107.6 18.0 %copy-start.45 = (f32[128]{0:T(128)}, f32[128]{0:T(128)S(1)}, u32[]{:S(2)}) copy-start(f32[128]{0:T(128)S(1)} %get-tuple-element.108) | copy-start | bytes 1540
  107.6 11.3 slice-start
  111.9 7.0 copy-start.6
  112.0 7.0 slice-start.1
  121.5 12.0 all-to-all-start.1
  130.2 10.4 copy-start.44
  137.2 12.7 copy-start.38
  142.8 12.9 copy-start.37
  158.0 11.5 all-to-all-start.2
  176.3 5.9 copy-start.23
  176.3 5.9 copy-start.22
  182.3 10.4 copy-start.39
  182.3 11.1 copy-start.35
  188.5 10.3 all-to-all-start.3
  192.6 98.1 %all-reduce.12.cloned.1.call-start = ((), (), s32[]{:S(2)}) async-start(), calls=%async_computation.40 | async-start | bytes 3145728
  205.9 7.7 copy-start.30
  213.6 4.4 copy-start.11
  228.4 98.4 %reduce-scatter.18.cloned.1.call-start = ((), (), s32[]{:S(2)}) async-start(), calls=%async_computation.18 | async-start | bytes 1769472 | tf_op jit(solution)/shard_map/reduce_scatter | solution.py:324
  229.8 7.5 copy-start.25
  229.8 7.5 copy-start.26
  239.1 53.9 %copy-start.33 = (f32[128]{0:T(128)S(1)}, f32[128]{0:T(128)}, u32[]{:S(2)}) copy-start(f32[128]{0:T(128)} %copy-done.32) | copy-start | bytes 1540
  239.1 120.6 %reduce-scatter.26.cloned.1.call-start = ((), (), s32[]{:S(2)}) async-start(), calls=%async_computation.25 | async-start | bytes 1327104 | tf_op jit(solution)/shard_map/reduce_scatter | solution.py:372
  241.8 151.6 %reduce-scatter.24.cloned.1.call-start = ((), (), s32[]{:S(2)}) async-start(), calls=%async_computation.23 | async-start | bytes 1327104 | tf_op jit(solution)/shard_map/reduce_scatter | solution.py:369
  294.6 140.2 %reduce-scatter.30.cloned.1.call-start = ((), (), s32[]{:S(2)}) async-start(), calls=%async_computation.29 | async-start | bytes 3538944 | tf_op jit(solution)/shard_map/reduce_scatter | solution.py:384
  298.3 178.7 %reduce-scatter.28.cloned.1.call-start = ((), (), s32[]{:S(2)}) async-start(), calls=%async_computation.27 | async-start | bytes 3538944 | tf_op jit(solution)/shard_map/reduce_scatter | solution.py:381
  302.1 217.3 %reduce-scatter.32.cloned.1.call-start = ((), (), s32[]{:S(2)}) async-start(), calls=%async_computation.31 | async-start | bytes 3538944 | tf_op jit(solution)/shard_map/reduce_scatter | solution.py:387
  306.0 248.1 %reduce-scatter.22.cloned.1.call-start = ((), (), s32[]{:S(2)}) async-start(), calls=%async_computation.21 | async-start | bytes 1327104 | tf_op jit(solution)/shard_map/reduce_scatter | solution.py:366
  331.9 256.1 %reduce-scatter.20.cloned.1.call-start = ((), (), s32[]{:S(2)}) async-start(), calls=%async_computation.19 | async-start | bytes 1327104 | tf_op jit(solution)/shard_map/reduce_scatter | solution.py:363
  335.2 320.2 %all-reduce.14.cloned.1.call-start = ((), (), s32[]{:S(2)}) async-start(), calls=%async_computation.41 | async-start | bytes 3538944 | tf_op jit(solution)/shard_map/psum | solution.py:393
  588.0 140.2 %reduce-scatter.36.cloned.1.call-start = ((), (), s32[]{:S(2)}) async-start(), calls=%async_computation.35 | async-start | bytes 7077888 | tf_op jit(solution)/shard_map/reduce_scatter | solution.py:439
  594.1 205.0 %reduce-scatter.34.cloned.1.call-start = ((), (), s32[]{:S(2)}) async-start(), calls=%async_computation.33 | async-start | bytes 7077888 | tf_op jit(solution)/shard_map/reduce_scatter | solution.py:436
  600.7 269.3 %reduce-scatter.38.cloned.1.call-start = ((), (), s32[]{:S(2)}) async-start(), calls=%async_computation.37 | async-start | bytes 7077888 | tf_op jit(solution)/shard_map/reduce_scatter | solution.py:442
  606.9 294.5 %reduce-scatter.40.cloned.1.call-start = ((), (), s32[]{:S(2)}) async-start(), calls=%async_computation.39 | async-start | bytes 221184
  609.3 357.9 %all-gather.24.cloned.1.call-start = ((), (), s32[]{:S(2)}) async-start(), calls=%async_computation.26 | async-start | bytes 1327104 | tf_op jit(solution)/shard_map/all_gather | solution.py:416
  655.5 314.6 %all-gather.22.cloned.1.call-start = ((), (), s32[]{:S(2)}) async-start(), calls=%async_computation.24 | async-start | bytes 1327104 | tf_op jit(solution)/shard_map/all_gather | solution.py:413
  656.1 316.9 %all-gather.20.cloned.1.call-start = ((), (), s32[]{:S(2)}) async-start(), calls=%async_computation.22 | async-start | bytes 1327104 | tf_op jit(solution)/shard_map/all_gather | solution.py:410
  656.8 339.3 %all-gather.18.cloned.1.call-start = ((), (), s32[]{:S(2)}) async-start(), calls=%async_computation.20 | async-start | bytes 1327104 | tf_op jit(solution)/shard_map/all_gather | solution.py:407
  657.4 378.5 %all-gather.30.cloned.1.call-start = ((), (), s32[]{:S(2)}) async-start(), calls=%async_computation.32 | async-start | bytes 3538944 | tf_op jit(solution)/shard_map/all_gather | solution.py:431
  658.1 416.7 %all-gather.28.cloned.1.call-start = ((), (), s32[]{:S(2)}) async-start(), calls=%async_computation.30 | async-start | bytes 3538944 | tf_op jit(solution)/shard_map/all_gather | solution.py:428
  658.9 454.9 %all-gather.26.cloned.1.call-start = ((), (), s32[]{:S(2)}) async-start(), calls=%async_computation.28 | async-start | bytes 3538944 | tf_op jit(solution)/shard_map/all_gather | solution.py:425
  659.6 519.3 %all-gather.34.cloned.1.call-start = ((), (), s32[]{:S(2)}) async-start(), calls=%async_computation.36 | async-start | bytes 7077888 | tf_op jit(solution)/shard_map/all_gather | solution.py:450
  728.2 515.8 %all-gather.32.cloned.1.call-start = ((), (), s32[]{:S(2)}) async-start(), calls=%async_computation.34 | async-start | bytes 7077888 | tf_op jit(solution)/shard_map/all_gather | solution.py:447
  799.1 509.9 %all-gather.36.cloned.1.call-start = ((), (), s32[]{:S(2)}) async-start(), calls=%async_computation.38 | async-start | bytes 7077888 | tf_op jit(solution)/shard_map/all_gather | solution.py:453
  904.7 4.9 copy-start.12
  904.7 4.9 copy-start.19
  907.0 3.2 copy-start.13
  907.0 3.2 copy-start.17
  907.0 3.7 copy-start.9
  907.0 3.7 copy-start.15
  (16 other events, 21.4 us)
Sparse Core Ops, SparseCore 0:
  20.6 29.8 all-gather.13
  52.6 26.2 all-gather.15
  228.5 62.1 all-reduce.11
  293.4 33.2 reduce-scatter.17
  328.9 30.7 reduce-scatter.25
  362.4 30.9 reduce-scatter.23
  396.3 38.4 reduce-scatter.29
  437.7 39.3 reduce-scatter.27
  480.0 39.4 reduce-scatter.31
  522.2 31.8 reduce-scatter.21
  557.0 30.9 reduce-scatter.19
  591.8 63.6 all-reduce.13
  658.3 69.7 reduce-scatter.35
  730.9 68.1 reduce-scatter.33
  801.8 68.1 reduce-scatter.37
  872.7 28.6 reduce-scatter.39
  903.0 20.9 all-gather.23
  925.6 22.2 all-gather.21
  949.6 22.4 all-gather.19
  973.7 22.2 all-gather.17
  997.8 38.0 all-gather.29
  1037.6 37.1 all-gather.27
  1076.6 37.1 all-gather.25
  1115.3 63.5 all-gather.33
  1180.6 63.3 all-gather.31
  1245.6 63.3 all-gather.35
where the time goes:
time: 1330 us; the launch traced here: 1320 us
  waiting for transfers between devices  923 us (69%)
  matrix products  123 us (9%)
  other arithmetic  98.1 us (7%)
  local copies, waits for them, and re-layouts  81.3 us (6%)
  blocking collectives  64.3 us (5%)
  starting transfers between devices  18.6 us (1%)
  between operations  16.4 us (1%)
    unnamed x28, waiting for transfers between devices  81.6 us
    reduce_scatter x1, waiting for transfers between devices, per_device(): lax.psum_scatter(g_expert_down.astype(jnp.bfloat16), 'context', scatter_d...  70.9 us
    reduce_scatter x1, waiting for transfers between devices, per_device(): lax.psum_scatter(g_expert_gate.astype(jnp.bfloat16), 'context', scatter_d...  70.8 us
    reduce_scatter x1, waiting for transfers between devices, per_device(): lax.psum_scatter(g_expert_up.astype(jnp.bfloat16), 'context', scatter_dim...  68.5 us
    all_gather x1, waiting for transfers between devices, per_device(): lax.all_gather(expert_parts[1].astype(jnp.bfloat16), 'context', axis=1, t...  59.7 us
    all_gather x1, waiting for transfers between devices, per_device(): lax.all_gather(expert_parts[0].astype(jnp.bfloat16), 'context', axis=1, t...  55.7 us
    all_gather x1, waiting for transfers between devices, per_device(): lax.all_gather(expert_parts[2].astype(jnp.bfloat16), 'context', axis=1, t...  55.5 us
    psum x1, waiting for transfers between devices, per_device(): lax.psum(dense_parts[1].astype(jnp.bfloat16), 'expert').astype(jnp.float32)  46.1 us
  transfers between devices with their start and end apart: 30, of which 25 were waited for; matrix products, arithmetic and copies ran while one was open for 13% of the time, Pallas kernels for 0%

commit v1 on v0

v1 whole, which is shorter than its diff:
```python
import math

import jax
import jax.numpy as jnp
from jax import lax
from jax.sharding import PartitionSpec as P

HEADS = 12
HEAD = 64
TOP = 2
EPSILON = 1e-06
MASKED = -1e30
LANES = 128
BF = jnp.bfloat16
F32 = jnp.float32


def mm(a, b):
    return jnp.dot(a, b, preferred_element_type=F32)


def mm_t(a, b):
    return lax.dot_general(a, b, (((1,), (1,)), ((), ())), preferred_element_type=F32)


def tmm(a, b):
    return lax.dot_general(a, b, (((0,), (0,)), ((), ())), preferred_element_type=F32)


def rope_table(positions):
    half = HEAD // 2
    frequency = jnp.exp(jnp.arange(half, dtype=F32) * (-2.0 * math.log(10000.0) / HEAD))
    angles = positions.astype(F32)[:, None] * frequency[None, :]
    return jnp.cos(angles), jnp.sin(angles)


def rotate(values, cosines, sines, turning):
    rows = values.shape[0]
    v = values.reshape(rows, HEADS, HEAD)
    former, latter = v[..., : HEAD // 2], v[..., HEAD // 2 :]
    c, s = cosines[:, None, :], turning * sines[:, None, :]
    return jnp.concatenate([former * c - latter * s, latter * c + former * s], -1).reshape(rows, -1)


def heads_of(values):
    return values.reshape(values.shape[0], HEADS, HEAD)


def silu_parts(v):
    s = jax.nn.sigmoid(v)
    return v * s, s * (1.0 + v * (1.0 - s))


def split3(v):
    a = v.astype(BF)
    r = v - a.astype(F32)
    b = r.astype(BF)
    return a, b, (r - b.astype(F32)).astype(BF)


def per_device(
    tokens, segments, routes, attn_gain, w_query, w_key, w_value, w_out, ffn_gain, w_router,
    shared_gate, shared_up, shared_down, expert_gate, expert_up, expert_down, cotangent,
):
    _, stretch, width = tokens.shape
    n_expert = lax.axis_size("expert")
    n_context = lax.axis_size("context")
    chips = n_context // 2
    back = n_context // 4
    me_c = lax.axis_index("context")
    local = expert_gate.shape[0]
    experts = n_expert * local
    cap = (9 * stretch * TOP + 8 * experts - 1) // (8 * experts)
    hidden = shared_gate.shape[1]
    scale = HEAD ** (-0.5)
    pair_groups = [[2 * i, 2 * i + 1] for i in range(chips)]
    chip_groups = [[2 * i + k for i in range(chips)] for k in range(2)]
    swap = [(c, c ^ 1) for c in range(n_context)]

    def up(d):
        return [(c, c + 2 * d) for c in range(n_context - 2 * d)]

    def down(d):
        return [(c + 2 * d, c) for c in range(n_context - 2 * d)]

    def window(block, steps):
        mine = jnp.stack([block] + [lax.ppermute(block, "context", steps(d)) for d in range(1, back + 1)])
        other = lax.ppermute(mine, "context", swap)
        return jnp.concatenate([mine, other], 0)

    def window_blocks(sign):
        d = 2 * sign * jnp.arange(back + 1, dtype=jnp.int32)
        return jnp.concatenate([me_c + d, (me_c ^ 1) + d])

    def positions_of(blocks):
        return (blocks[:, None] * stretch + jnp.arange(stretch, dtype=jnp.int32)[None, :]).reshape(-1)

    tok = tokens[0]
    seg = segments[0]
    dy = cotangent[0]
    dyf = dy.astype(F32)
    seg_rows = jnp.pad(seg[None, :].astype(BF), ((0, 7), (0, width - stretch)))
    packet = jnp.concatenate([tok, seg_rows], 0)
    low_win = window(packet, up)
    high_win = window(packet, down)
    nwin = 2 * (back + 1)

    def unpack(win):
        return win[:, :stretch].reshape(nwin * stretch, width), win[:, stretch, :stretch].astype(jnp.int32).reshape(-1)

    low_tok, low_seg = unpack(low_win)
    high_tok, high_seg = unpack(high_win)
    low_pos = positions_of(window_blocks(-1))
    high_pos = positions_of(window_blocks(1))
    own_pos = me_c * stretch + jnp.arange(stretch, dtype=jnp.int32)
    gain_a = attn_gain.astype(F32)
    gain_b = ffn_gain.astype(F32)

    def norm_in(rows):
        x = rows.astype(F32)
        return (x * lax.rsqrt(jnp.mean(x * x, -1, keepdims=True) + EPSILON) * gain_a).astype(BF)

    low_na = norm_in(low_tok)
    na = low_na[:stretch]
    kw = rotate(mm(low_na, w_key), *rope_table(low_pos), 1.0).astype(BF)
    vw = mm(low_na, w_value).astype(BF)
    q = rotate(mm(na, w_query), *rope_table(own_pos), 1.0).astype(BF)
    scores = jnp.einsum("qhd,khd->hqk", heads_of(q), heads_of(kw), preferred_element_type=F32) * scale
    allowed = (seg[:, None] == low_seg[None, :]) & (low_pos[None, :] <= own_pos[:, None]) & (low_pos[None, :] >= 0)
    scores = jnp.where(allowed[None], scores, MASKED)
    peak = jnp.max(scores, -1, keepdims=True)
    e = jnp.where(allowed[None], jnp.exp(scores - peak), 0.0)
    total = jnp.sum(e, -1, keepdims=True)
    lse = (peak + jnp.log(total))[..., 0].T
    att_f = (jnp.einsum("hqk,khd->qhd", e.astype(BF), heads_of(vw), preferred_element_type=F32) / total[..., 0].T[..., None]).reshape(stretch, width)
    att = att_f.astype(BF)
    tokf = tok.astype(F32)
    h1 = tokf + mm(att, w_out)
    rstd_b = lax.rsqrt(jnp.mean(h1 * h1, -1, keepdims=True) + EPSILON)
    n_b = h1 * rstd_b
    nb = (n_b * gain_b).astype(BF)

    assigned = routes[0].reshape(stretch * TOP)
    onehot = (assigned[:, None] == jnp.arange(experts, dtype=jnp.int32)[None, :])
    row_i = jnp.arange(stretch * TOP, dtype=jnp.int32)
    earlier = (row_i[:, None] > row_i[None, :]).astype(BF)
    before = mm(earlier, onehot.astype(BF))
    place = jnp.sum(jnp.where(onehot, before, 0.0), -1).astype(jnp.int32)
    slot = jnp.where(place < cap, assigned * cap + place, experts * cap).reshape(stretch, TOP)
    slots = experts * cap
    slot_i = jnp.arange(slots, dtype=jnp.int32)
    pick = [(slot_i[:, None] == slot[None, :, r]) for r in range(TOP)]
    pick_b = [p.astype(BF) for p in pick]
    pick_any = (pick[0] | pick[1]).astype(BF)

    logits = mm(nb, w_router)
    route_hot = (routes[0][:, :, None] == jnp.arange(experts, dtype=jnp.int32))
    chosen = jnp.sum(jnp.where(route_hot, logits[:, None, :], 0.0), -1)
    gates = jax.nn.softmax(chosen, -1)

    gate_cols = jnp.stack([jnp.stack(split3(gates[:, r]), -1) for r in range(TOP)])
    gate_cols = jnp.pad(gate_cols, ((0, 0), (0, 0), (0, LANES - 3)))
    out_rows = mm(pick_any, nb).astype(BF)
    out_gates = (mm(pick_b[0], gate_cols[0]) + mm(pick_b[1], gate_cols[1])).astype(BF)
    outgoing = jnp.concatenate([out_rows, out_gates], -1).reshape(n_expert, local * cap, width + LANES)
    x_in = lax.all_to_all(outgoing, "expert", 0, 0, tiled=True)
    dy_out = mm(pick_any, dy).astype(BF).reshape(n_expert, local * cap, width)
    dy_in = lax.all_to_all(dy_out, "expert", 0, 0, tiled=True)

    def by_expert(rows):
        lead = rows.shape[:-2]
        r = rows.reshape((-1, local, cap, rows.shape[-1]))
        return jnp.moveaxis(r, 1, 0).reshape(local, -1, rows.shape[-1])

    def from_expert(rows):
        return jnp.moveaxis(rows.reshape(local, n_expert, cap, rows.shape[-1]), 0, 1).reshape(n_expert, local * cap, rows.shape[-1])

    def d_out_of(xg, dyr):
        g = jnp.sum(xg[..., width : width + 3].astype(F32), -1, keepdims=True)
        return xg[..., :width], (g * dyr.astype(F32)).astype(BF)

    def expert_core(x, d_out, wg, wu, wd):
        eg, eu = mm(x, wg), mm(x, wu)
        act, slope = silu_parts(eg)
        eh = (act * eu).astype(BF)
        d_eh = mm_t(d_out, wd)
        return eh, (d_eh * eu * slope).astype(BF), (d_eh * act).astype(BF)

    xg = by_expert(x_in)
    dyr = by_expert(dy_in)
    outs, dins = [], []
    for i in range(local):
        x, d_out = d_out_of(xg[i], dyr[i])
        eh, d_eg, d_eu = expert_core(x, d_out, expert_gate[i], expert_up[i], expert_down[i])
        outs.append(mm(eh, expert_down[i]).astype(BF))
        dins.append((mm_t(d_eg, expert_gate[i]) + mm_t(d_eu, expert_up[i])).astype(BF))
    ret = from_expert(jnp.concatenate([jnp.stack(outs), jnp.stack(dins)], -1))
    ret = lax.all_to_all(ret, "expert", 0, 0, tiled=True).reshape(slots, 2 * width)

    x_all = by_expert(lax.all_gather(x_in, "context", axis=0, tiled=True))
    dy_all = by_expert(lax.all_gather(dy_in, "context", axis=0, tiled=True))
    rows_all = x_all.shape[1]
    piece = rows_all
    while piece > 1152:
        piece //= 2

    def expert_grads(i):
        def term(carry, k):
            xs = lax.dynamic_slice_in_dim(x_all[i], k * piece, piece, 0)
            ds = lax.dynamic_slice_in_dim(dy_all[i], k * piece, piece, 0)
            x, d_out = d_out_of(xs, ds)
            eh, d_eg, d_eu = expert_core(x, d_out, expert_gate[i], expert_up[i], expert_down[i])
            new = (tmm(x, d_eg), tmm(x, d_eu), tmm(eh, d_out))
            return (new if carry is None else tuple(a + b for a, b in zip(carry, new))), None

        if piece == rows_all:
            return term(None, 0)[0]
        zero = tuple(jnp.zeros(s.shape[1:], F32) for s in (expert_gate, expert_up, expert_down))
        return lax.scan(term, zero, jnp.arange(rows_all // piece))[0]

    eg_grads = [expert_grads(i) for i in range(local)]
    g_expert = tuple(jnp.stack([g[j] for g in eg_grads]) for j in range(3))

    sg, su = mm(nb, shared_gate), mm(nb, shared_up)
    act, slope = silu_parts(sg)
    hs = (act * su).astype(BF)
    shared_out = mm(hs, shared_down)
    d_hs = mm_t(dy, shared_down)
    d_sg = (d_hs * su * slope).astype(BF)
    d_su = (d_hs * act).astype(BF)
    d_b = mm_t(d_sg, shared_gate) + mm_t(d_su, shared_up)

    part = hidden // n_context
    nb_all = lax.all_gather(nb, "context", axis=0, tiled=True)
    dy_seq = lax.all_gather(dy, "context", axis=0, tiled=True)
    wg_s = lax.dynamic_slice_in_dim(shared_gate, me_c * part, part, 1)
    wu_s = lax.dynamic_slice_in_dim(shared_up, me_c * part, part, 1)
    wd_s = lax.dynamic_slice_in_dim(shared_down, me_c * part, part, 0)
    hs_s, dsg_s, dsu_s = expert_core(nb_all, dy_seq, wg_s, wu_s, wd_s)
    gate_s, up_s, down_s = tmm(nb_all, dsg_s), tmm(nb_all, dsu_s), tmm(hs_s, dy_seq)
    rows_of = lambda a: a.astype(BF).reshape(-1, part if a.shape[1] == part else width)
    flat = jnp.concatenate([gate_s.astype(BF).reshape(-1), up_s.astype(BF).reshape(-1), down_s.astype(BF).reshape(-1)]).reshape(n_expert, -1, LANES)
    mine = jnp.sum(lax.all_to_all(flat, "expert", 0, 0, tiled=True).astype(F32), 0).astype(BF)
    whole = lax.all_gather(mine[None], ("context", "expert"), axis=0, tiled=True).reshape(n_context, 3, -1)
    g_sg = jnp.moveaxis(whole[:, 0].reshape(n_context, width, part), 0, 1).reshape(width, hidden).astype(F32)
    g_su = jnp.moveaxis(whole[:, 1].reshape(n_context, width, part), 0, 1).reshape(width, hidden).astype(F32)
    g_sd = whole[:, 2].reshape(hidden, width).astype(F32)

    back_all = [tmm(p, ret) for p in pick_b]
    rows_back = [b[:, :width] for b in back_all]
    moe = gates[:, :1] * rows_back[0] + gates[:, 1:] * rows_back[1]
    result = (h1 + shared_out + moe).astype(BF)
    d_gate = jnp.stack([jnp.sum(dyf * r, -1) for r in rows_back], -1)
    d_chosen = gates * (d_gate - jnp.sum(gates * d_gate, -1, keepdims=True))
    d_logit = jnp.sum(jnp.where(route_hot, d_chosen[..., None], 0.0), 1)
    g_router = lax.dot_general(nb.astype(F32), d_logit, (((0,), (0,)), ((), ())), precision=lax.Precision.HIGHEST)
    d_b = d_b + lax.dot_general(d_logit, w_router.astype(F32), (((1,), (1,)), ((), ())), precision=lax.Precision.HIGHEST)
    d_b = d_b + back_all[0][:, width:] + back_all[1][:, width:]
    g_ffn = jnp.sum(d_b * n_b, 0)
    d_nb = d_b * gain_b
    d_h1 = dyf + rstd_b * (d_nb - n_b * jnp.mean(d_nb * n_b, -1, keepdims=True))
    d_attn = d_h1.astype(BF)
    g_out = tmm(att, d_attn)
    d_att = mm_t(d_attn, w_out).astype(BF)
    delta = jnp.sum(heads_of(d_att.astype(F32) * att_f), -1)

    stats = jnp.concatenate(list(split3(lse)[:2]) + list(split3(delta)[:2]), -1)
    stats = jnp.pad(stats, ((0, 0), (0, LANES - stats.shape[-1])))
    high_d = window(jnp.concatenate([d_attn, stats], -1), down).reshape(nwin * stretch, width + LANES)

    def grads_of(queries, keys, values, d_attended, log_sum, dlt, mask):
        s = jnp.einsum("qhd,khd->hqk", heads_of(queries), heads_of(keys), preferred_element_type=F32) * scale
        p = jnp.where(mask[None], jnp.exp(jnp.where(mask[None], s - log_sum.T[..., None], 0.0)), 0.0)
        dp = jnp.einsum("qhd,khd->hqk", heads_of(d_attended), heads_of(values), preferred_element_type=F32)
        return p.astype(BF), (p * (dp - dlt.T[..., None])).astype(BF)

    _, ds = grads_of(q, kw, vw, d_att, lse, delta, allowed)
    d_q = scale * jnp.einsum("hqk,khd->qhd", ds, heads_of(kw), preferred_element_type=F32).reshape(stretch, width)
    own_rope = rope_table(own_pos)
    d_q_pre = rotate(d_q, *own_rope, -1.0).astype(BF)

    high_q = rotate(mm(norm_in(high_tok), w_query), *rope_table(high_pos), 1.0).astype(BF)
    st = high_d[:, width:].astype(F32)
    high_lse = st[:, :HEADS] + st[:, HEADS : 2 * HEADS]
    high_delta = st[:, 2 * HEADS : 3 * HEADS] + st[:, 3 * HEADS : 4 * HEADS]
    high_datt = mm_t(high_d[:, :width], w_out).astype(BF)
    mask = (high_seg[:, None] == seg[None, :]) & (own_pos[None, :] <= high_pos[:, None]) & (high_pos[:, None] < n_context * stretch)
    k_own, v_own = kw[:stretch], vw[:stretch]
    p2, ds2 = grads_of(high_q, k_own, v_own, high_datt, high_lse, high_delta, mask)
    d_k = scale * jnp.einsum("hqk,qhd->khd", ds2, heads_of(high_q), preferred_element_type=F32).reshape(stretch, width)
    d_v = jnp.einsum("hqk,qhd->khd", p2, heads_of(high_datt), preferred_element_type=F32).reshape(stretch, width)
    d_k_pre = rotate(d_k, *own_rope, -1.0).astype(BF)
    d_v_low = d_v.astype(BF)
    g_q, g_k, g_v = tmm(na, d_q_pre), tmm(na, d_k_pre), tmm(na, d_v_low)
    d_a = mm_t(d_q_pre, w_query) + mm_t(d_k_pre, w_key) + mm_t(d_v_low, w_value)
    rstd_a = lax.rsqrt(jnp.mean(tokf * tokf, -1, keepdims=True) + EPSILON)
    n_a = tokf * rstd_a
    g_attn = jnp.sum(d_a * n_a, 0)
    d_na = d_a * gain_a
    d_tokens = d_h1 + rstd_a * (d_na - n_a * jnp.mean(d_na * n_a, -1, keepdims=True))

    def scatter(x, axis, groups, n):
        parts = x.reshape((n, x.shape[0] // n) + x.shape[1:])
        got = lax.all_to_all(parts, axis, 0, 0, axis_index_groups=groups, tiled=True)
        return jnp.sum(got.astype(F32), 0).astype(BF)

    def spread(x, axis, groups, n):
        parts = jnp.broadcast_to(x[None], (n,) + x.shape)
        got = lax.all_to_all(parts, axis, 0, 0, axis_index_groups=groups, tiled=True)
        return got.reshape((n * x.shape[0],) + x.shape[1:])

    def reduce_all(x):
        x = scatter(x, "context", pair_groups, 2)
        x = scatter(x, "expert", None, n_expert)
        x = scatter(x, "context", chip_groups, chips)
        x = spread(x, "context", chip_groups, chips)
        x = spread(x, "expert", None, n_expert)
        return spread(x, "context", pair_groups, 2)

    small = jnp.concatenate([g_attn[None], g_ffn[None], g_router.T], 0)
    small = jnp.pad(small, ((0, 256 - small.shape[0]), (0, 0)))
    first = reduce_all(g_out.astype(BF)).astype(F32)
    last = reduce_all(jnp.concatenate([g_q, g_k, g_v, small], 0).astype(BF)).astype(F32)
    g_q, g_k, g_v, small = last[:width], last[width : 2 * width], last[2 * width : 3 * width], last[3 * width :]
    return (
        result[None], d_tokens[None], small[0], g_q, g_k, g_v, first, small[1],
        small[2 : 2 + experts].T, g_sg, g_su, g_sd, g_expert[0], g_expert[1], g_expert[2],
    )


def solution(mesh):
    rows = P("expert", "context", None)
    owned = P("expert", None, None)
    placed = (rows, P("expert", "context"), rows) + (P(),) * 10 + (owned,) * 3 + (rows,)
    return jax.shard_map(
        per_device, mesh=mesh, in_specs=placed,
        out_specs=(rows, rows) + (P(),) * 10 + (owned,) * 3, check_vma=False,
    )
```

time: 1330 us -> 772 us (0.58)
  waiting for transfers between devices: 923 us -> 75.5 us
  matrix products: 123 us -> 241 us
  other arithmetic: 98.1 us -> 172 us
  local copies, waits for them, and re-layouts: 81.3 us -> 147 us
  starting transfers between devices: 18.6 us -> 68.1 us
  blocking collectives: 64.3 us -> 39.7 us
    reduce_scatter x11 -> x0, waiting for transfers between devices: 479 us -> none  [the longest x1 70.9 us: per_device(): lax.psum_scatter(g_expert_down.astype(jnp.bfloat16), 'context', scatter_d...]
    all_gather x12 -> x5, waiting for transfers between devices: 304 us -> 0.05 us  [the longest x1 0.02 us: per_device(): dy_all = by_expert(lax.all_gather(dy_in, 'context', axis=0, tiled=True))]
    dot_general x39 -> x66, matrix products: 123 us -> 241 us  [the longest x15 96 us: tmm(): lax.dot_general(a, b, (((0,), (0,)), ((), ())), preferred_element_type=F32)]
    unnamed x28 -> x5, waiting for transfers between devices: 81.6 us -> 0.08 us
    psum x1 -> x0, waiting for transfers between devices: 46.1 us -> none  [per_device(): lax.psum(dense_parts[1].astype(jnp.bfloat16), 'expert').astype(jnp.float32)]
    all_to_all x0 -> x4, blocking collectives: none -> 39.7 us  [the longest x2 22.7 us: spread(): lax.all_to_all(parts, axis, 0, 0, axis_index_groups=groups, tiled=True)]
    another operation x3 -> x12, other arithmetic: 2.62 us -> 41.4 us  [the longest x3 33.3 us: per_device(): g_expert = tuple((jnp.stack([g[j] for g in eg_grads]) for j in range(3)))]
    all_to_all x4 -> x12, waiting for transfers between devices: 11.6 us -> 48.8 us  [the longest x4 26.8 us: scatter(): lax.all_to_all(parts, axis, 0, 0, axis_index_groups=groups, tiled=True)]
  transfers between devices with their start and end apart: 30 -> 26, of which waited for: 25 -> 9; matrix products, arithmetic and copies ran while one was open for 13% -> 59% of each run, Pallas kernels for 0% -> 0%
where the time goes in v1:
time: 772 us; the launch traced here: 759 us
  matrix products  241 us (31%)
  other arithmetic  172 us (22%)
  local copies, waits for them, and re-layouts  147 us (19%)
  waiting for transfers between devices  75.5 us (10%)
  starting transfers between devices  68.1 us (9%)
  blocking collectives  39.7 us (5%)
  between operations  16.1 us (2%)
    dot_general x15, matrix products, tmm(): lax.dot_general(a, b, (((0,), (0,)), ((), ())), preferred_element_type=F32)  96 us
    dot_general x26, matrix products, mm(): return jnp.dot(a, b, preferred_element_type=F32)  71.2 us
    convert_element_type x1, other arithmetic, per_device(): g_sd = whole[:, 2].reshape(hidden, width).astype(F32)  62.2 us
    dot_general x17, matrix products, mm_t(): lax.dot_general(a, b, (((1,), (1,)), ((), ())), preferred_element_type=F32)  47.1 us
    another operation x3, other arithmetic, per_device(): g_expert = tuple((jnp.stack([g[j] for g in eg_grads]) for j in range(3)))  33.3 us
    convert_element_type x12, local copies, waits for them, and re-layouts, d_out_of(): return (xg[..., :width], (g * dyr.astype(F32)).astype(BF))  31.9 us
    all_to_all x4, waiting for transfers between devices, scatter(): lax.all_to_all(parts, axis, 0, 0, axis_index_groups=groups, tiled=True)  26.8 us
    unnamed x229, local copies, waits for them, and re-layouts  26.7 us
  transfers between devices with their start and end apart: 26, of which 9 were waited for; matrix products, arithmetic and copies ran while one was open for 59% of the time, Pallas kernels for 0%

profile of v1, /device:TPU:0, one launch (start us, length us, event | category | flops | bytes accessed | tf_op | source)
XLA Modules:
  0.0 759.3 jit_solution(1306876091852791170)
XLA Ops:
  11.1 7.7 %collective-permute-start.1 = (bf16[136,768]{1,0:T(8,128)(2,1)}, bf16[136,768]{1,0:T(8,128)(2,1)}, u32[]{:S(2)}, u32[]{:S(2)}) collective-permute-start(bf16[136,768]{1,0:T(8,128)(2,1)} %get-tuple-element.61), channel_id=1, source_target_pairs={{0,4},{1,5},{2,6},{3,7},{8,12},{9,13},{10,14},{11,15},{16,20},{17,... | collective-permute-start | bytes 626696 | tf_op jit(solution)/shard_map/ppermute | solution.py:87
  18.8 4.8 collective-permute-start
  27.1 9.2 %collective-permute-done.4 = bf16[136,768]{1,0:T(8,128)(2,1)} collective-permute-done((bf16[136,768]{1,0:T(8,128)(2,1)}, bf16[136,768]{1,0:T(8,128)(2,1)}, u32[]{:S(2)}, u32[]{:S(2)}) %collective-permute-start.4) | collective-permute-done | bytes 208928 | tf_op jit(solution)/shard_map/ppermute | solution.py:87
  71.0 4.1 all-to-all-start.1
  82.3 4.1 fusion.221
  102.7 4.1 all-to-all-start
  113.8 3.0 fusion.181
  168.2 4.2 all-to-all-start.2
  173.8 4.5 convolution_add_fusion.4
  178.3 6.5 all-to-all-done.2
  208.4 5.5 all_to_all.80
  216.4 4.1 all-to-all-start.10
  220.6 16.2 %collective-permute-done.7 = bf16[128,896]{1,0:T(8,128)(2,1)} collective-permute-done((bf16[128,896]{1,0:T(8,128)(2,1)}, bf16[128,896]{1,0:T(8,128)(2,1)}, u32[]{:S(2)}, u32[]{:S(2)}) %collective-permute-start.7) | collective-permute-done | bytes 229408 | tf_op jit(solution)/shard_map/ppermute | solution.py:87
  238.9 6.5 fusion.130
  247.2 4.0 all-to-all-start.11
  252.9 5.2 all-to-all-done.11
  261.1 4.2 all-to-all-start.12
  273.9 4.4 fusion.147
  278.3 7.3 fusion.128
  294.7 11.5 %all_to_all.81 = bf16[2,1280,768]{2,1,0:T(8,128)(2,1)} all-to-all(bf16[2,1280,768]{2,1,0:T(8,128)(2,1)} %bitcast.338), channel_id=1, replica_groups={{0,1},{2,3},{4,5},{6,7},{8,9},{10,11},{12,13},{14,15},{16,17},{18,19},{..., dimensions={0} | all-to-all | bytes 7864320 | tf_op jit(solution)/shard_map/all_to_all | solution.py:304
  308.0 4.1 all-to-all-start.13
  312.2 3.1 fusion.103
  315.3 4.7 reduce_sum.292
  320.0 3.0 fusion.206
  323.0 4.7 all-to-all-start.4
  337.5 2.8 fusion.119
  341.3 9.8 %all-to-all-done.4 = bf16[4,320,768]{2,1,0:T(8,128)(2,1)S(1)} async-done(((bf16[4,320,768]{2,1,0:T(8,128)(2,1)}), bf16[4,320,768]{2,1,0:T(8,128)(2,1)S(1)}, u32[]{:S(2)}, u32[]{:S(2)}) %all-to-all-start.4) | async-done | bytes 1966112 | tf_op jit(solution)/shard_map/all_to_all | solution.py:304
  353.3 3.6 all-to-all-start.14
  359.1 5.1 all-to-all-start.5
  366.5 11.8 %all-to-all-done.5 = bf16[4,80,768]{2,1,0:T(8,128)(2,1)S(1)} async-done(((bf16[4,80,768]{2,1,0:T(8,128)(2,1)}), bf16[4,80,768]{2,1,0:T(8,128)(2,1)S(1)}, u32[]{:S(2)}, u32[]{:S(2)}) %all-to-all-start.5) | async-done | bytes 491552 | tf_op jit(solution)/shard_map/all_to_all | solution.py:304
  378.3 3.5 all-to-all-start.15
  381.9 14.5 %all-to-all-done.15 = bf16[4,1152,128]{2,1,0:T(8,128)(2,1)S(1)} async-done(((bf16[4,1152,128]{2,1,0:T(8,128)(2,1)}), bf16[4,1152,128]{2,1,0:T(8,128)(2,1)S(1)}, u32[]{:S(2)}, u32[]{:S(2)}) %all-to-all-start.15) | async-done | bytes 1179680 | tf_op jit(solution)/shard_map/all_to_all | solution.py:243
  396.4 15.6 %all_to_all.82 = bf16[4,80,768]{2,1,0:T(8,128)(2,1)S(1)} all-to-all(bf16[4,80,768]{2,1,0:T(8,128)(2,1)S(1)} %broadcast_in_dim.118), channel_id=1, replica_groups={{0,2,4,6},{1,3,5,7},{8,10,12,14},{9,11,13,15},{16,18,20,22},{17,19,21,2..., dimensions={0} | all-to-all | bytes 983040 | tf_op jit(solution)/shard_map/all_to_all | solution.py:309
  413.5 3.6 all-to-all-start.7
  417.2 4.2 fusion.162
  425.4 2.8 copy.204
  431.2 4.0 copy.209
  435.1 4.7 reshape.866
  439.9 6.0 copy.210
  445.9 4.7 reshape.867
  450.9 7.1 all_to_all.83
  460.0 3.1 fusion.313
  471.3 10.2 %fusion.32 = f32[1152,2048]{1,0:T(8,128)} fusion(bf16[2,768,2048]{2,1,0:T(8,128)(2,1)} %param.30, bf16[1152,896]{1,0:T(8,128)(2,1)} %squeeze.84), kind=kOutput, calls=%fused_computation.59 | convolution fusion | flops 3623878656 | bytes 14352384 | tf_op jit(solution)/shard_map/dot_general | solution.py:19
  485.3 10.0 %fusion.50 = f32[1152,2048]{1,0:T(8,128)} fusion(bf16[2,768,2048]{2,1,0:T(8,128)(2,1)} %param.30, bf16[1152,896]{1,0:T(8,128)(2,1)} %squeeze.83), kind=kOutput, calls=%fused_computation.77 | convolution fusion | flops 3623878656 | bytes 14352384 | tf_op jit(solution)/shard_map/dot_general | solution.py:19
  495.6 3.4 multiply_convert_fusion.29
  505.8 10.3 %fusion.20 = f32[1152,2048]{1,0:T(8,128)} fusion(bf16[1152,768]{1,0:T(8,128)(2,1)} %convert_element_type.565, bf16[2,2048,768]{2,1,0:T(8,128)(2,1)} %param.32), kind=kOutput, calls=%fused_computation.47 | convolution fusion | flops 3623878656 | bytes 14352384 | tf_op jit(solution)/shard_map/dot_general | solution.py:23
  516.1 8.3 %fusion.38 = f32[1152,2048]{1,0:T(8,128)} fusion(bf16[1152,768]{1,0:T(8,128)(2,1)S(1)} %copy-done.40, bf16[2,2048,768]{2,1,0:T(8,128)(2,1)} %param.32), kind=kOutput, calls=%fused_computation.65 | convolution fusion | flops 3623878656 | bytes 14352384 | tf_op jit(solution)/shard_map/dot_general | solution.py:23
  524.4 11.2 %fusion.15 = f32[1,768,2048]{2,1,0:T(8,128)} fusion(f32[1152,2048]{1,0:T(8,128)} %fusion.20, f32[1152,2048]{1,0:T(8,128)S(1)} %bitcast.399, bf16[1152,896]{1,0:T(8,128)(2,1)S(1)} %copy-done.32), kind=kOutput, calls=%fused_computation.38 | convolution fusion | flops 3638034432 | bytes 26935296 | tf_op jit(solution)/shard_map/dot_general | solution.py:27
  535.6 13.5 %fusion.16 = f32[1,768,2048]{2,1,0:T(8,128)} fusion(f32[1152,2048]{1,0:T(8,128)} %fusion.38, f32[1152,2048]{1,0:T(8,128)} %fusion.50, bf16[1152,896]{1,0:T(8,128)(2,1)S(1)} %copy-done.33), kind=kOutput, calls=%fused_computation.39 | convolution fusion | flops 3638034432 | bytes 26935296 | tf_op jit(solution)/shard_map/dot_general | solution.py:27
  549.1 11.6 %pad_maximum_fusion.1 = f32[2,768,2048]{2,1,0:T(8,128)} fusion(f32[1,768,2048]{2,1,0:T(8,128)} %fusion.15, f32[1,768,2048]{2,1,0:T(8,128)} %fusion.16), kind=kLoop, calls=%fused_computation.1 | loop fusion | flops 3145728 | bytes 25165824 | tf_op jit(solution)/shard_map/stack | solution.py:222
  560.7 8.0 %fusion.26 = f32[1152,2048]{1,0:T(8,128)} fusion(bf16[2,768,2048]{2,1,0:T(8,128)(2,1)} %param.31, bf16[1152,896]{1,0:T(8,128)(2,1)S(1)} %copy-done.32), kind=kOutput, calls=%fused_computation.53 | convolution fusion | flops 3623878656 | bytes 14352384 | tf_op jit(solution)/shard_map/dot_general | solution.py:19
  568.7 8.4 %fusion.44 = f32[1152,2048]{1,0:T(8,128)} fusion(bf16[2,768,2048]{2,1,0:T(8,128)(2,1)} %param.31, bf16[1152,896]{1,0:T(8,128)(2,1)S(1)} %copy-done.33), kind=kOutput, calls=%fused_computation.71 | convolution fusion | flops 3623878656 | bytes 14352384 | tf_op jit(solution)/shard_map/dot_general | solution.py:19
  577.2 14.4 %fusion.13 = f32[1,2048,768]{2,1,0:T(8,128)} fusion(f32[1152,2048]{1,0:T(8,128)} %fusion.26, f32[1152,768]{1,0:T(8,128)S(1)} %copy-done.23, f32[1152]{0:T(1024)S(1)} %convert_reduce_fusion, f32[1152,2048]{1,0:T(8,128)} %fusion.32), kind=kOutput, calls=%fused_computation.36 | convolution fusion | flops 3639803904 | bytes 28709376 | tf_op jit(solution)/shard_map/dot_general | solution.py:27
  591.6 14.3 %fusion.14 = f32[1,2048,768]{2,1,0:T(8,128)} fusion(f32[1152,2048]{1,0:T(8,128)} %fusion.44, f32[1152,768]{1,0:T(8,128)S(1)} %copy-done.22, f32[1152]{0:T(1024)S(1)} %convert_reduce_fusion.1, f32[1152,2048]{1,0:T(8,128)} %fusion.50), kind=kOutput, calls=%fused_computation.37 | convolution fusion | flops 3639803904 | bytes 28709376 | tf_op jit(solution)/shard_map/dot_general | solution.py:27
  605.9 10.2 %pad_maximum_fusion.2 = f32[2,2048,768]{2,1,0:T(8,128)} fusion(f32[1,2048,768]{2,1,0:T(8,128)} %fusion.13, f32[1,2048,768]{2,1,0:T(8,128)} %fusion.14), kind=kLoop, calls=%fused_computation.2 | loop fusion | flops 3145728 | bytes 25165824 | tf_op jit(solution)/shard_map/stack | solution.py:222
  616.1 14.5 %fusion.11 = f32[1,768,2048]{2,1,0:T(8,128)} fusion(f32[1152,2048]{1,0:T(8,128)} %fusion.32, f32[1152,2048]{1,0:T(8,128)} %fusion.20, f32[1152,2048]{1,0:T(8,128)} %fusion.26, bf16[1152,896]{1,0:T(8,128)(2,1)S(1)} %copy-done.32), kind=kOutput, calls=%fused_computation.34 | convolution fusion | flops 3647471616 | bytes 36372480 | tf_op jit(solution)/shard_map/dot_general | solution.py:27
  630.6 14.4 %fusion.12 = f32[1,768,2048]{2,1,0:T(8,128)} fusion(f32[1152,2048]{1,0:T(8,128)} %fusion.50, f32[1152,2048]{1,0:T(8,128)} %fusion.38, f32[1152,2048]{1,0:T(8,128)} %fusion.44, bf16[1152,896]{1,0:T(8,128)(2,1)S(1)} %copy-done.33), kind=kOutput, calls=%fused_computation.35 | convolution fusion | flops 3647471616 | bytes 36372480 | tf_op jit(solution)/shard_map/dot_general | solution.py:27
  645.0 11.6 %pad_maximum_fusion = f32[2,768,2048]{2,1,0:T(8,128)} fusion(f32[1,768,2048]{2,1,0:T(8,128)} %fusion.11, f32[1,768,2048]{2,1,0:T(8,128)} %fusion.12), kind=kLoop, calls=%fused_computation | loop fusion | flops 3145728 | bytes 25165824 | tf_op jit(solution)/shard_map/stack | solution.py:222
  656.6 11.5 %reshape.855 = bf16[8,3,196608]{2,1,0:T(4,128)(2,1)} reshape(bf16[36864,128]{1,0:T(8,128)(2,1)} %all-gather.16.cloned.1.call-done) | data formatting | bytes 18874368 | tf_op jit(solution)/shard_map/reshape | solution.py:244
  668.1 62.2 %fusion.2 = (f32[8,196608]{1,0:T(8,128)}, f32[8,196608]{1,0:T(8,128)}, f32[8,196608]{1,0:T(8,128)}) fusion(bf16[8,3,196608]{2,1,0:T(4,128)(2,1)} %reshape.855), kind=kLoop, calls=%fused_computation.16 | loop fusion | flops 4718592 | bytes 28311552 | tf_op jit(solution)/shard_map/convert_element_type | solution.py:247
  730.4 6.4 reshape.865
  736.8 4.8 copy.222
  741.6 4.1 copy.215
  748.7 3.7 copy.214
  (453 shorter events, 228.5 us)
Async XLA Ops:
  7.2 99.7 %copy-start = (bf16[768,2048]{1,0:T(8,128)(2,1)S(1)}, bf16[768,2048]{1,0:T(8,128)(2,1)}, u32[]{:S(2)}) copy-start(bf16[768,2048]{1,0:T(8,128)(2,1)} %param.27) | copy-start | bytes 9437188
  7.2 32.1 %copy-start.95 = (bf16[768]{0:T(1024)(128)(2,1)S(1)}, bf16[768]{0:T(1024)(128)(2,1)}, u32[]{:S(2)}) copy-start(bf16[768]{0:T(1024)(128)(2,1)} %param.20) | copy-start | bytes 4612
  7.2 32.1 %copy-start.96 = (bf16[768]{0:T(1024)(128)(2,1)S(1)}, bf16[768]{0:T(1024)(128)(2,1)}, u32[]{:S(2)}) copy-start(bf16[768]{0:T(1024)(128)(2,1)} %param.25) | copy-start | bytes 4612
  7.2 304.9 %all-gather.14.cloned.1.call-start = ((), (), s32[]{:S(2)}) async-start(), calls=%async_computation.19 | async-start | bytes 1769472 | tf_op jit(solution)/shard_map/all_gather | solution.py:235
  9.8 16.2 %collective-permute-start.3 = (bf16[136,768]{1,0:T(8,128)(2,1)}, bf16[136,768]{1,0:T(8,128)(2,1)}, u32[]{:S(2)}, u32[]{:S(2)}) collective-permute-start(bf16[136,768]{1,0:T(8,128)(2,1)} %get-tuple-element.61), channel_id=1, source_target_pairs={{2,0},{3,1},{4,2},{5,3},{6,4},{7,5},{10,8},{11,9},{12,10},{13,11},... | collective-permute-start | bytes 626696 | tf_op jit(solution)/shard_map/ppermute | solution.py:87
  11.1 14.9 %collective-permute-start.1 = (bf16[136,768]{1,0:T(8,128)(2,1)}, bf16[136,768]{1,0:T(8,128)(2,1)}, u32[]{:S(2)}, u32[]{:S(2)}) collective-permute-start(bf16[136,768]{1,0:T(8,128)(2,1)} %get-tuple-element.61), channel_id=1, source_target_pairs={{0,4},{1,5},{2,6},{3,7},{8,12},{9,13},{10,14},{11,15},{16,20},{17,... | collective-permute-start | bytes 626696 | tf_op jit(solution)/shard_map/ppermute | solution.py:87
  18.8 8.3 %collective-permute-start = (bf16[136,768]{1,0:T(8,128)(2,1)}, bf16[136,768]{1,0:T(8,128)(2,1)}, u32[]{:S(2)}, u32[]{:S(2)}) collective-permute-start(bf16[136,768]{1,0:T(8,128)(2,1)} %get-tuple-element.61), channel_id=1, source_target_pairs={{0,2},{1,3},{2,4},{3,5},{4,6},{5,7},{8,10},{9,11},{10,12},{11,13},... | collective-permute-start | bytes 626696 | tf_op jit(solution)/shard_map/ppermute | solution.py:87
  23.6 12.7 %collective-permute-start.4 = (bf16[136,768]{1,0:T(8,128)(2,1)}, bf16[136,768]{1,0:T(8,128)(2,1)}, u32[]{:S(2)}, u32[]{:S(2)}) collective-permute-start(bf16[136,768]{1,0:T(8,128)(2,1)} %get-tuple-element.61), channel_id=1, source_target_pairs={{4,0},{5,1},{6,2},{7,3},{12,8},{13,9},{14,10},{15,11},{20,16},{21,... | collective-permute-start | bytes 626696 | tf_op jit(solution)/shard_map/ppermute | solution.py:87
  24.9 295.0 %all-gather.8.cloned.1.call-start = ((), (), s32[]{:S(2)}) async-start(), calls=%async_computation.16 | async-start | bytes 1769472 | tf_op jit(solution)/shard_map/all_gather | solution.py:234
  25.1 14.1 %copy-start.98 = (s32[6]{0:T(128)}, s32[6]{0:T(128)S(1)}, u32[]{:S(2)}) copy-start(s32[6]{0:T(128)S(1)} %add_multiply_fusion.1) | copy-start | bytes 76
  38.7 5.7 collective-permute-start.5
  38.7 5.7 collective-permute-start.2
  39.3 11.1 %copy-start.67 = (f32[768]{0:T(1024)}, f32[768]{0:T(1024)S(1)}, u32[]{:S(2)}) copy-start(f32[768]{0:T(1024)S(1)} %convert_element_type.458) | copy-start | bytes 9220
  42.3 10.1 %copy-start.93 = (s32[128]{0:T(128)}, s32[128]{0:T(128)S(1)}, u32[]{:S(2)}) copy-start(s32[128]{0:T(128)S(1)} %get-tuple-element.108) | copy-start | bytes 1540
  52.5 4.7 copy-start.59
  71.0 15.4 %all-to-all-start.1 = ((bf16[4,72,768]{2,1,0:T(8,128)(2,1)}), bf16[4,72,768]{2,1,0:T(8,128)(2,1)}, u32[]{:S(2)}, u32[]{:S(2)}) async-start(bf16[4,72,768]{2,1,0:T(8,128)(2,1)} %bitcast.365), calls=%async_computation.1 | async-start | bytes 884736 | tf_op jit(solution)/shard_map/all_to_all | solution.py:168
  75.2 350.2 %all-gather.12.cloned.1.call-start = ((), (), s32[]{:S(2)}) async-start(), calls=%async_computation.18 | async-start | bytes 3981312 | tf_op jit(solution)/shard_map/all_gather | solution.py:201
  102.7 17.7 %all-to-all-start = ((bf16[4,72,896]{2,1,0:T(8,128)(2,1)}), bf16[4,72,896]{2,1,0:T(8,128)(2,1)}, u32[]{:S(2)}, u32[]{:S(2)}) async-start(bf16[4,72,896]{2,1,0:T(8,128)(2,1)} %bitcast.354), calls=%async_computation | async-start | bytes 1032192 | tf_op jit(solution)/shard_map/all_to_all | solution.py:166
  109.0 9.2 %copy-start.52 = (f32[128,2048]{1,0:T(8,128)}, f32[128,2048]{1,0:T(8,128)S(1)}, u32[]{:S(2)}) copy-start(f32[128,2048]{1,0:T(8,128)S(1)} %fusion.318) | copy-start | bytes 3145732
  109.6 8.6 %copy-start.53 = (f32[128,2048]{1,0:T(8,128)}, f32[128,2048]{1,0:T(8,128)S(1)}, u32[]{:S(2)}) copy-start(f32[128,2048]{1,0:T(8,128)S(1)} %fusion.319) | copy-start | bytes 3145732
  113.8 4.4 copy-start.54
  147.1 8.2 %slice-start.2 = ((s8[6291456]{0:T(1024)(128)(4,1)}), s8[4194304]{0:T(1024)(128)(4,1)S(1)}, s32[]{:S(2)}) async-start(s8[6291456]{0:T(1024)(128)(4,1)} %bitcast.341), calls=%async_computation.23 | async-start | bytes 8388608
  149.8 5.5 slice-start.3
  152.6 5.1 slice-start.6
  168.2 16.6 %all-to-all-start.2 = ((bf16[4,72,1536]{2,1,0:T(8,128)(2,1)}), bf16[4,72,1536]{2,1,0:T(8,128)(2,1)}, u32[]{:S(2)}, u32[]{:S(2)}) async-start(bf16[4,72,1536]{2,1,0:T(8,128)(2,1)} %copy.186), calls=%async_computation.2 | async-start | bytes 1769472 | tf_op jit(solution)/shard_map/all_to_all | solution.py:198
  172.5 290.7 %all-gather.10.cloned.1.call-start = ((), (), s32[]{:S(2)}) async-start(), calls=%async_computation.17 | async-start | bytes 4644864 | tf_op jit(solution)/shard_map/all_gather | solution.py:200
  184.8 4.2 copy-start.82
  184.9 4.2 copy-start.58
  184.9 4.2 copy-start.65
  184.9 4.2 copy-start.71
  184.9 4.2 copy-start.86
  201.3 19.3 %collective-permute-start.6 = (bf16[128,896]{1,0:T(8,128)(2,1)}, bf16[128,896]{1,0:T(8,128)(2,1)}, u32[]{:S(2)}, u32[]{:S(2)}) collective-permute-start(bf16[128,896]{1,0:T(8,128)(2,1)} %get-tuple-element.56), channel_id=1, source_target_pairs={{2,0},{3,1},{4,2},{5,3},{6,4},{7,5},{10,8},{11,9},{12,10},{13,11},... | collective-permute-start | bytes 688136 | tf_op jit(solution)/shard_map/ppermute | solution.py:87
  202.6 34.2 %collective-permute-start.7 = (bf16[128,896]{1,0:T(8,128)(2,1)}, bf16[128,896]{1,0:T(8,128)(2,1)}, u32[]{:S(2)}, u32[]{:S(2)}) collective-permute-start(bf16[128,896]{1,0:T(8,128)(2,1)} %get-tuple-element.56), channel_id=1, source_target_pairs={{4,0},{5,1},{6,2},{7,3},{12,8},{13,9},{14,10},{15,11},{20,16},{21,... | collective-permute-start | bytes 688136 | tf_op jit(solution)/shard_map/ppermute | solution.py:87
  216.4 29.0 %all-to-all-start.10 = ((bf16[4,96,768]{2,1,0:T(8,128)(2,1)}), bf16[4,96,768]{2,1,0:T(8,128)(2,1)}, u32[]{:S(2)}, u32[]{:S(2)}) async-start(bf16[4,96,768]{2,1,0:T(8,128)(2,1)} %bitcast.353), calls=%async_computation.10 | async-start | bytes 1179648 | tf_op jit(solution)/shard_map/all_to_all | solution.py:304
  238.9 26.4 %collective-permute-start.8 = (bf16[3,128,896]{2,1,0:T(8,128)(2,1)}, bf16[3,128,896]{2,1,0:T(8,128)(2,1)}, u32[]{:S(2)}, u32[]{:S(2)}) collective-permute-start(bf16[3,128,896]{2,1,0:T(8,128)(2,1)} %pad_maximum_fusion.13), channel_id=1, source_target_pairs={{0,1},{1,0},{2,3},{3,2},{4,5},{5,4},{6,7},{7,6},{8,9},{9,8},{10,11... | collective-permute-start | bytes 2064392 | tf_op jit(solution)/shard_map/ppermute | solution.py:88
  247.2 10.9 %all-to-all-start.11 = ((bf16[4,24,768]{2,1,0:T(8,128)(2,1)}), bf16[4,24,768]{2,1,0:T(8,128)(2,1)}, u32[]{:S(2)}, u32[]{:S(2)}) async-start(bf16[4,24,768]{2,1,0:T(8,128)(2,1)} %bitcast.377), calls=%async_computation.11 | async-start | bytes 294912 | tf_op jit(solution)/shard_map/all_to_all | solution.py:304
  261.1 33.6 %all-to-all-start.12 = ((bf16[4,24,768]{2,1,0:T(8,128)(2,1)}), bf16[4,24,768]{2,1,0:T(8,128)(2,1)}, u32[]{:S(2)}, u32[]{:S(2)}) async-start(bf16[4,24,768]{2,1,0:T(8,128)(2,1)} %broadcast_in_dim.210), calls=%async_computation.12 | async-start | bytes 294912 | tf_op jit(solution)/shard_map/all_to_all | solution.py:309
  308.0 15.0 %all-to-all-start.13 = ((bf16[4,96,768]{2,1,0:T(8,128)(2,1)}), bf16[4,96,768]{2,1,0:T(8,128)(2,1)}, u32[]{:S(2)}, u32[]{:S(2)}) async-start(bf16[4,96,768]{2,1,0:T(8,128)(2,1)} %broadcast_in_dim.212), calls=%async_computation.13 | async-start | bytes 1179648 | tf_op jit(solution)/shard_map/all_to_all | solution.py:309
  323.0 4.7 copy-start.49
  323.0 28.2 %all-to-all-start.4 = ((bf16[4,320,768]{2,1,0:T(8,128)(2,1)}), bf16[4,320,768]{2,1,0:T(8,128)(2,1)S(1)}, u32[]{:S(2)}, u32[]{:S(2)}) async-start(bf16[4,320,768]{2,1,0:T(8,128)(2,1)} %bitcast.340), calls=%async_computation.4 | async-start | bytes 3932160 | tf_op jit(solution)/shard_map/all_to_all | solution.py:304
  353.3 5.8 all-to-all-start.14
  359.1 19.2 %copy-start.12 = (bf16[2,384,768]{2,1,0:T(8,128)(2,1)}, bf16[2,384,768]{2,1,0:T(8,128)(2,1)S(1)}, u32[]{:S(2)}) copy-start(bf16[2,384,768]{2,1,0:T(8,128)(2,1)S(1)} %all-to-all-done.14) | copy-start | bytes 3538948
  359.1 19.2 %all-to-all-start.5 = ((bf16[4,80,768]{2,1,0:T(8,128)(2,1)}), bf16[4,80,768]{2,1,0:T(8,128)(2,1)S(1)}, u32[]{:S(2)}, u32[]{:S(2)}) async-start(bf16[4,80,768]{2,1,0:T(8,128)(2,1)} %bitcast.357), calls=%async_computation.5 | async-start | bytes 983040 | tf_op jit(solution)/shard_map/all_to_all | solution.py:304
  378.3 18.1 %all-to-all-start.15 = ((bf16[4,1152,128]{2,1,0:T(8,128)(2,1)}), bf16[4,1152,128]{2,1,0:T(8,128)(2,1)S(1)}, u32[]{:S(2)}, u32[]{:S(2)}) async-start(bf16[4,1152,128]{2,1,0:T(8,128)(2,1)} %bitcast.346), calls=%async_computation.15 | async-start | bytes 2359296 | tf_op jit(solution)/shard_map/all_to_all | solution.py:243
  396.4 17.1 %copy-start.19 = (bf16[4,1152,128]{2,1,0:T(8,128)(2,1)}, bf16[4,1152,128]{2,1,0:T(8,128)(2,1)S(1)}, u32[]{:S(2)}) copy-start(bf16[4,1152,128]{2,1,0:T(8,128)(2,1)S(1)} %all-to-all-done.15) | copy-start | bytes 3538948
  413.5 37.2 %all-to-all-start.7 = ((bf16[4,320,768]{2,1,0:T(8,128)(2,1)}), bf16[4,320,768]{2,1,0:T(8,128)(2,1)S(1)}, u32[]{:S(2)}, u32[]{:S(2)}) async-start(bf16[4,320,768]{2,1,0:T(8,128)(2,1)} %broadcast_in_dim.120), calls=%async_computation.7 | async-start | bytes 3932160 | tf_op jit(solution)/shard_map/all_to_all | solution.py:309
  417.1 239.5 %all-gather.16.cloned.1.call-start = ((), (), s32[]{:S(2)}) async-start(), calls=%async_computation.20 | async-start | bytes 9732096 | tf_op jit(solution)/shard_map/all_gather | solution.py:244
  417.1 4.3 copy-start.7
  417.1 4.3 copy-start.11
  417.1 4.3 copy-start.26
  417.2 4.3 copy-start.43
  417.2 4.3 copy-start.66
  417.2 4.3 copy-start.87
  417.2 4.3 copy-start.92
  471.3 10.2 %copy-start.5 = (bf16[1,32,36,896]{3,1,2,0:T(8,128)(2,1)S(1)}, bf16[1,32,36,896]{3,1,2,0:T(8,128)(2,1)}, u32[]{:S(2)}) copy-start(bf16[1,32,36,896]{3,1,2,0:T(8,128)(2,1)} %get-tuple-element.33) | copy-start | bytes 6193156
  505.8 10.3 %copy-start.40 = (bf16[1152,768]{1,0:T(8,128)(2,1)S(1)}, bf16[1152,768]{1,0:T(8,128)(2,1)}, u32[]{:S(2)}) copy-start(bf16[1152,768]{1,0:T(8,128)(2,1)} %convert_element_type.560) | copy-start | bytes 5308420
  505.8 18.6 %slice-start.8 = ((s8[9437184]{0:T(1024)(128)(4,1)}), s8[4194304]{0:T(1024)(128)(4,1)S(1)}, s32[]{:S(2)}) async-start(s8[9437184]{0:T(1024)(128)(4,1)} %bitcast.398), calls=%async_computation.29 | async-start | bytes 8388608
  505.8 18.6 %slice-start.9 = ((s8[9437184]{0:T(1024)(128)(4,1)}), s8[4194304]{0:T(1024)(128)(4,1)S(1)}, s32[]{:S(2)}) async-start(s8[9437184]{0:T(1024)(128)(4,1)} %bitcast.398), calls=%async_computation.30 | async-start | bytes 8388608
  516.1 8.3 %copy-start.32 = (bf16[1152,896]{1,0:T(8,128)(2,1)S(1)}, bf16[1152,896]{1,0:T(8,128)(2,1)}, u32[]{:S(2)}) copy-start(bf16[1152,896]{1,0:T(8,128)(2,1)} %squeeze.84) | copy-start | bytes 6193156
  516.1 8.3 %slice-start.10 = ((s8[9437184]{0:T(1024)(128)(4,1)}), s8[1048576]{0:T(1024)(128)(4,1)S(1)}, s32[]{:S(2)}) async-start(s8[9437184]{0:T(1024)(128)(4,1)} %bitcast.398), calls=%async_computation.31 | async-start | bytes 2097152
  524.4 11.2 %copy-start.33 = (bf16[1152,896]{1,0:T(8,128)(2,1)S(1)}, bf16[1152,896]{1,0:T(8,128)(2,1)}, u32[]{:S(2)}) copy-start(bf16[1152,896]{1,0:T(8,128)(2,1)} %squeeze.83) | copy-start | bytes 6193156
  568.7 8.4 %copy-start.23 = (f32[1152,768]{1,0:T(8,128)S(1)}, f32[1152,768]{1,0:T(8,128)}, u32[]{:S(2)}) copy-start(f32[1152,768]{1,0:T(8,128)} %reshape.867) | copy-start | bytes 10616836
  577.2 14.4 %copy-start.22 = (f32[1152,768]{1,0:T(8,128)S(1)}, f32[1152,768]{1,0:T(8,128)}, u32[]{:S(2)}) copy-start(f32[1152,768]{1,0:T(8,128)} %reshape.866) | copy-start | bytes 10616836
  741.6 5.0 slice-start.1
  (73 other events, 159.1 us)
Sparse Core Ops, SparseCore 0:
  25.1 26.9 all-gather.13
  61.6 23.3 all-gather.7
  88.6 40.1 all-gather.11
  178.4 59.4 all-gather.9
  425.5 82.8 all-gather.15
